TPU v7x, 256 devices: a whole 4x4x8 slice. The times are simulated.
256 devices in a mesh: gx: 32 (over z, x), yz: 8 (over y, core).
Axes of the slice: x: 4, y: 4, z: 8, core: 2. Of those that a mesh axis runs over, the one named last changes fastest.
Arguments:
- tensor_slabs: bfloat16 [2048, 32, 1024], P('gx', 'yz'), may hold values from -6 to 6
- slab_counts: int32 [8], replicated, may hold values from 1 to 4, 16 in all
- column_scale: float32 [16, 1024], replicated, may hold values from -6 to 6
- samples: int32 [16, 256], replicated, may hold values from 0 to 1023
Outputs:
- basis_factor: float32 [2048, 256], P('gx')
- core_tensor: bfloat16 [256, 32, 1024], P(None, 'yz', 'gx')
Inputs may be any that keep to these rules, and one draw needn't show every extreme that they name: `slab_counts`: the counts sum to 16; the largest is exactly 4. Slots at or beyond an index's count hold no slab and are not read.
All inputs are finite; a program needn't handle non-finite values.
Results may differ from a plain program's by a relative error of at most 0.0057.
Values may be sent and summed in bfloat16 or wider, within the bound.
No kernel may reach another device: no remote copies, remote signals or barrier semaphores. Data moves between devices by JAX's collectives and lax.ppermute only.
A program may use at most 64 MiB of HBM per device.

v0:
```python
import math

import jax
import jax.numpy as jnp
from jax import lax
from jax.sharding import PartitionSpec as P


def from_everyone(array, axis):
    copies = jnp.broadcast_to(array, (lax.axis_size(axis), *array.shape))
    return lax.all_to_all(copies, axis, split_axis=0, concat_axis=0, tiled=True)


def of_everyone(array, axis):
    return from_everyone(array, axis).sum(axis=0)


def rows_for(lines, devices):
    spare = -lines.shape[0] % devices
    if not spare:
        return lines
    return jnp.concatenate([lines, jnp.zeros((spare, *lines.shape[1:]), lines.dtype)])


def laid_out(parts, dim):
    dims = list(parts.shape[1:])
    dims[dim] *= parts.shape[0]
    return jnp.moveaxis(parts, 0, dim).reshape(dims)


def gathered_copies(array, axis, dim):
    parts = from_everyone(array, axis)
    return laid_out(parts, dim)


def in_blocks(array, dim, devices):
    dims = array.shape
    parts = array.reshape(*dims[:dim], devices, dims[dim] // devices, *dims[dim + 1 :])
    return jnp.moveaxis(parts, dim, 0)


def sum_at_owner(array, axis, dim):
    parts = in_blocks(array, dim, lax.axis_size(axis))
    arrived = lax.all_to_all(parts, axis, split_axis=0, concat_axis=0, tiled=True)
    return arrived.sum(axis=0)


def nested_sum(array, axes):
    lines = array.reshape(-1, array.shape[-1])
    padded = rows_for(lines, lax.axis_size(axes))
    whole = gathered_copies(sum_at_owner(padded, axes, 0), axes, 0)
    return lax.slice_in_dim(whole, 0, len(lines)).reshape(array.shape)


def hadamard_columns(picked, length):
    index_rows = jnp.arange(length, dtype=jnp.int32)[:, None]
    picked_row = picked[None, :]
    parity = jnp.zeros((length, picked.shape[0]), jnp.int32)
    for bit_place in range(length.bit_length() - 1):
        parity = parity + jnp.bitwise_and(
            jnp.right_shift(index_rows, bit_place), 1
        ) * jnp.bitwise_and(jnp.right_shift(picked_row, bit_place), 1)
    return (1 - 2 * (parity % 2)).astype(jnp.bfloat16)


def local(tensor_slabs, slab_counts, column_scale, samples):
    row_count, slot_count, column_width = tensor_slabs.shape
    sketch_width = samples.shape[1]
    total_slabs = column_scale.shape[0]
    own_index = lax.axis_index("yz")
    group_numbers = jnp.arange(slab_counts.shape[0], dtype=jnp.int32)
    offset = jnp.sum(jnp.where(group_numbers < own_index, slab_counts, 0))
    own_count = slab_counts[own_index]
    pad_scale = jnp.concatenate(
        [column_scale, jnp.zeros((slot_count, column_width), column_scale.dtype)], 0
    )
    pad_samples = jnp.concatenate([samples, jnp.zeros((slot_count, sketch_width), jnp.int32)], 0)
    own_scale = lax.dynamic_slice_in_dim(pad_scale, offset, slot_count, 0)
    own_samples = lax.dynamic_slice_in_dim(pad_samples, offset, slot_count, 0)

    def add_slab(position, total):
        alive = (position < own_count).astype(jnp.float32)
        piece = lax.dynamic_index_in_dim(tensor_slabs, position, 1, keepdims=False)
        slab_scale = lax.dynamic_index_in_dim(own_scale, position, 0, keepdims=False)
        scaled = (piece.astype(jnp.float32) * slab_scale[None, :]).astype(jnp.bfloat16)
        hadamard_part = hadamard_columns(
            lax.dynamic_index_in_dim(own_samples, position, 0, keepdims=False), column_width
        )
        return total + alive * jnp.dot(scaled, hadamard_part, preferred_element_type=jnp.float32)

    partial_sketch = lax.fori_loop(
        0, slot_count, add_slab, jnp.zeros((row_count, sketch_width), jnp.float32)
    )
    normalizer = 1.0 / math.sqrt(total_slabs * column_width)
    sketch = of_everyone(partial_sketch, "yz") * normalizer
    gram_matrix = nested_sum(jnp.dot(sketch.T, sketch, precision=lax.Precision.HIGHEST), "gx")
    cholesky_factor = jnp.linalg.cholesky(gram_matrix)
    basis_factor = lax.linalg.triangular_solve(
        cholesky_factor, sketch, left_side=False, lower=True, transpose_a=True
    )
    factor_bf = basis_factor.astype(jnp.bfloat16)
    moved = lax.all_to_all(tensor_slabs, "gx", split_axis=2, concat_axis=0, tiled=True)
    every_row = gathered_copies(factor_bf, "gx", 0)
    flattened = moved.reshape(moved.shape[0], moved.shape[1] * moved.shape[2])
    combined = jnp.dot(every_row.T, flattened, preferred_element_type=jnp.float32).reshape(
        sketch_width, moved.shape[1], moved.shape[2]
    )
    slot_alive = (jnp.arange(slot_count, dtype=jnp.int32) < own_count).astype(jnp.float32)
    core_tensor = (combined * slot_alive[None, :, None]).astype(jnp.bfloat16)
    return (basis_factor, core_tensor)


def solution(mesh):
    placed = (P("gx", "yz", None), P(), P(), P())
    return jax.shard_map(
        local,
        mesh=mesh,
        in_specs=placed,
        out_specs=(P("gx", None), P(None, "yz", "gx")),
        check_vma=False,
    )
```

profile of v0, /device:TPU:2, one launch (start us, length us, event | category | flops | bytes accessed | tf_op | source)
XLA Modules:
  0.0 178.3 jit_solution(11258716550988022247)
XLA Ops:
  0.7 1.3 fusion.44
  5.1 0.9 pad_dynamic-slice_fusion
  5.9 14.3 %while.18 = (s32[]{:T(128)}, f32[64,256]{1,0:T(8,128)S(1)}, s32[]{:T(128)}, bf16[64,4,1024]{2,1,0:T(4,128)(2,1)}, f32[4,1024]{1,0:T(4,128)S(1)}, /*index=5*/s32[4,256]{1,0:T(4,128)S(1)}, s32[]{:T(128)}, s32[]{:T(128)}) while((s32[]{:T(128)}, f32[64,256]{1,0:T(8,128)S(1)}, s32[]{:T(128)}, bf16[64,4,1024]{2,1,0:T(4,128)(2,1)}, ...), condition=%wide.region_2.3_spmd.clone, body=%wide.region_1.2_spmd.clone.sunk | while | flops 42476548 | bytes 904325 | solution.py:91
  6.6 1.3 dynamic-slice_convert_fusion.2
  7.9 1.6 fusion.60
  10.2 1.3 dynamic-slice_convert_fusion.2
  11.5 1.6 fusion.60
  13.8 1.3 dynamic-slice_convert_fusion.2
  15.1 1.6 fusion.60
  17.4 1.3 dynamic-slice_convert_fusion.2
  18.6 1.6 fusion.60
  20.3 14.5 %all_to_all.35 = f32[8,64,256]{2,1,0:T(8,128)S(1)} all-to-all(f32[8,64,256]{2,1,0:T(8,128)S(1)} %broadcast_in_dim.28), channel_id=1, replica_groups=mesh['gx'=32,'yz'=8] {'yz'}, dimensions={0} | all-to-all | bytes 1048576 | tf_op jit(solution)/shard_map/all_to_all | solution.py:11
  35.3 22.3 %all_to_all.36 = f32[32,8,256]{2,1,0:T(8,128)S(1)} all-to-all(f32[32,8,256]{2,1,0:T(8,128)S(1)} %convolution_bitcast_fusion), channel_id=1, replica_groups=mesh['gx'=32,'yz'=8] {'gx'}, dimensions={0} | all-to-all | bytes 524288 | tf_op jit(solution)/shard_map/all_to_all | solution.py:44
  57.6 0.7 broadcast_in_dim.29
  58.3 5.6 %all-to-all-start.2 = ((f32[32,8,256]{2,1,0:T(8,128)}), f32[32,8,256]{2,1,0:T(8,128)S(1)}, u32[]{:S(2)}, u32[]{:S(2)}) async-start(f32[32,8,256]{2,1,0:T(8,128)} %broadcast_in_dim.29), calls=%async_computation.2 | async-start | bytes 524288 | tf_op jit(solution)/shard_map/all_to_all | solution.py:11
  63.9 0.8 copy.18
  64.8 1.5 reshape.139
  66.3 7.9 %all-to-all-done.2 = f32[32,8,256]{2,1,0:T(8,128)S(1)} async-done(((f32[32,8,256]{2,1,0:T(8,128)}), f32[32,8,256]{2,1,0:T(8,128)S(1)}, u32[]{:S(2)}, u32[]{:S(2)}) %all-to-all-start.2) | async-done | bytes 262176 | tf_op jit(solution)/shard_map/all_to_all | solution.py:11
  74.2 5.8 %all-to-all-start.4 = ((bf16[32,2,4096]{2,1,0:T(2,128)(2,1)}), bf16[32,2,4096]{2,1,0:T(2,128)(2,1)S(1)}, u32[]{:S(2)}, u32[]{:S(2)}) async-start(bf16[32,2,4096]{2,1,0:T(2,128)(2,1)} %reshape.139), calls=%async_computation.4 | async-start | bytes 1048576 | tf_op jit(solution)/shard_map/all_to_all | solution.py:102
  80.2 11.7 %cholesky.50 = f32[128,128]{1,0:T(8,128)S(1)} custom-call(f32[128,128]{1,0:T(8,128)S(1)} %cholesky.118), custom_call_target="Cholesky" | custom-call | tf_op jit(solution)/shard_map/jit(cholesky)/cholesky | solution.py:97
  92.0 9.8 %custom-call.14 = f32[1,128,128]{1,2,0:T(8,128)S(1)} custom-call(f32[1,128,128]{2,1,0:T(8,128)S(1)} %get-tuple-element.235), custom_call_target="InvertDiagBlocksLowerTriangular" | custom-call | tf_op jit(solution)/shard_map/jit(cholesky)/cholesky | solution.py:97
  102.3 11.7 %cholesky.105 = f32[128,128]{1,0:T(8,128)S(1)} custom-call(f32[128,128]{1,0:T(8,128)S(1)} %convolution_subtract_fusion), custom_call_target="Cholesky" | custom-call | tf_op jit(solution)/shard_map/jit(cholesky)/cholesky | solution.py:97
  116.0 3.8 %while.17 = (s32[]{:T(128)}, f32[256,256]{1,0:T(8,128)S(1)}, s32[2,2]{1,0:T(2,128)S(1)}, f32[2,128,128]{2,1,0:T(8,128)S(1)}, s32[]{:T(128)}) while((s32[]{:T(128)}, f32[256,256]{1,0:T(8,128)S(1)}, s32[2,2]{1,0:T(2,128)S(1)}, f32[2,128,128]{2,1,0:T(8,128)S(1)}, s32[]{:T(128)}) %tuple.94), condition=%wide.while_cond, body=%wide.while_body.sunk | while | flops 2 | bytes 131189 | solution.py:98
  116.6 1.3 bitcast_dynamic-update-slice_fusion.2
  118.5 1.3 bitcast_dynamic-update-slice_fusion.2
  119.8 19.9 %custom-call.15 = f32[2,128,128]{1,2,0:T(8,128)S(1)} custom-call(f32[2,128,128]{2,1,0:T(8,128)S(1)} %get-tuple-element.165), custom_call_target="InvertDiagBlocksLowerTriangular" | custom-call | tf_op jit(solution)/shard_map/triangular_solve | solution.py:98
  141.0 1.1 broadcast_in_dim.30
  142.1 9.9 %all-to-all-start.3 = ((bf16[32,64,256]{2,1,0:T(8,128)(2,1)}), bf16[32,64,256]{2,1,0:T(8,128)(2,1)S(1)}, u32[]{:S(2)}, u32[]{:S(2)}) async-start(bf16[32,64,256]{2,1,0:T(8,128)(2,1)} %broadcast_in_dim.30), calls=%async_computation.3 | async-start | bytes 2097152 | tf_op jit(solution)/shard_map/all_to_all | solution.py:11
  152.5 0.7 reshape.140
  153.8 0.8 reshape.116
  154.6 22.8 %all-to-all-done.3 = bf16[32,64,256]{2,1,0:T(8,128)(2,1)S(1)} async-done(((bf16[32,64,256]{2,1,0:T(8,128)(2,1)}), bf16[32,64,256]{2,1,0:T(8,128)(2,1)S(1)}, u32[]{:S(2)}, u32[]{:S(2)}) %all-to-all-start.3) | async-done | bytes 1048608 | tf_op jit(solution)/shard_map/all_to_all | solution.py:11
  177.4 0.9 fusion.35
  (71 shorter events, 7.0 us)
Async XLA Ops:
  0.6 4.4 %copy-start.1 = (s32[16,256]{1,0:T(8,128)S(1)}, s32[16,256]{1,0:T(8,128)}, u32[]{:S(2)}) copy-start(s32[16,256]{1,0:T(8,128)} %param.9) | copy-start | bytes 49156
  3.2 0.7 copy-start.2
  57.6 6.3 %copy-start = (bf16[64,4,1024]{2,1,0:T(4,128)(2,1)S(1)}, bf16[64,4,1024]{2,1,0:T(4,128)(2,1)}, u32[]{:S(2)}) copy-start(bf16[64,4,1024]{2,1,0:T(4,128)(2,1)} %get-tuple-element.387) | copy-start | bytes 1572868
  58.3 15.9 %all-to-all-start.2 = ((f32[32,8,256]{2,1,0:T(8,128)}), f32[32,8,256]{2,1,0:T(8,128)S(1)}, u32[]{:S(2)}, u32[]{:S(2)}) async-start(f32[32,8,256]{2,1,0:T(8,128)} %broadcast_in_dim.29), calls=%async_computation.2 | async-start | bytes 524288 | tf_op jit(solution)/shard_map/all_to_all | solution.py:11
  74.2 66.8 %all-to-all-start.4 = ((bf16[32,2,4096]{2,1,0:T(2,128)(2,1)}), bf16[32,2,4096]{2,1,0:T(2,128)(2,1)S(1)}, u32[]{:S(2)}, u32[]{:S(2)}) async-start(bf16[32,2,4096]{2,1,0:T(2,128)(2,1)} %reshape.139), calls=%async_computation.4 | async-start | bytes 1048576 | tf_op jit(solution)/shard_map/all_to_all | solution.py:102
  142.1 35.3 %all-to-all-start.3 = ((bf16[32,64,256]{2,1,0:T(8,128)(2,1)}), bf16[32,64,256]{2,1,0:T(8,128)(2,1)S(1)}, u32[]{:S(2)}, u32[]{:S(2)}) async-start(bf16[32,64,256]{2,1,0:T(8,128)(2,1)} %broadcast_in_dim.30), calls=%async_computation.3 | async-start | bytes 2097152 | tf_op jit(solution)/shard_map/all_to_all | solution.py:11
where the time goes:
time: 179 us; the launch traced here: 178 us
  other arithmetic  61.8 us (35%)
  blocking collectives  36.8 us (21%)
  waiting for transfers between devices  30.8 us (17%)
  starting transfers between devices  21.2 us (12%)
  local copies, waits for them, and re-layouts  12.3 us (7%)
  matrix products  8.79 us (5%)
  between operations  3.94 us (2%)
  loops' own time  2.63 us (1%)
    another operation x6, other arithmetic, local(): cholesky_factor = jnp.linalg.cholesky(gram_matrix)  33.9 us
    all_to_all x2, waiting for transfers between devices, from_everyone(): return lax.all_to_all(copies, axis, split_axis=0, concat_axis=0, tiled=True)  30.8 us
    all_to_all x1, blocking collectives, sum_at_owner(): lax.all_to_all(parts, axis, split_axis=0, concat_axis=0, tiled=True)  22.3 us
    another operation x3, other arithmetic, local(): lax.linalg.triangular_solve(cholesky_factor, sketch, left_side=False, low...  19.9 us
    all_to_all x2, starting transfers between devices, from_everyone(): return lax.all_to_all(copies, axis, split_axis=0, concat_axis=0, tiled=True)  15.4 us
    all_to_all x1, blocking collectives, from_everyone(): return lax.all_to_all(copies, axis, split_axis=0, concat_axis=0, tiled=True)  14.5 us
    dot_general x4, matrix products, add_slab(): jnp.dot(scaled, hadamard_part, preferred_element_type=jnp.float32)  6.37 us
    all_to_all x1, starting transfers between devices, local(): lax.all_to_all(tensor_slabs, 'gx', split_axis=2, concat_axis=0, tiled=True)  5.78 us
  transfers between devices with their start and end apart: 3, of which 2 were waited for; matrix products, arithmetic and copies ran while one was open for 36% of the time, Pallas kernels for 0%

commit v1 on v0

v1 whole, which is shorter than its diff:
```python
import functools

import jax
import jax.numpy as jnp
from jax import lax
from jax.experimental import pallas as pl
from jax.experimental.pallas import tpu as pltpu
from jax.sharding import PartitionSpec as P

F32, BF16, I32 = jnp.float32, jnp.bfloat16, jnp.int32
NN, NT, TN = ((1,), (0,)), ((1,), (1,)), ((0,), (0,))
HIGHEST = lax.Precision.HIGHEST
AHEAD = 10
BLOCK = 64


def dot(a, b, dims, precision=None):
    return lax.dot_general(
        a, b, (dims, ((), ())), precision=precision, preferred_element_type=F32
    )


def signs(rows, picked):
    both = lax.broadcasted_iota(I32, (rows, picked.shape[1]), 0) & picked
    both = both ^ (both >> 4)
    both = both ^ (both >> 2)
    both = both ^ (both >> 1)
    return (1 - 2 * (both & 1)).astype(F32)


def own_slabs(counts_ref, index, groups):
    offset = jnp.int32(0)
    for group in range(groups):
        offset = offset + jnp.where(group < index, counts_ref[group], 0)
    return offset, counts_ref[index]


def sketch_kernel(tensor_ref, counts_ref, scale_ref, samples_ref, keep_ref, send_ref, moved_ref,
                  hadamard_ref, total_ref):
    rows, slots, width = tensor_ref.shape
    total_slabs, sketch = samples_ref.shape
    index = lax.axis_index("yz")
    offset, count = own_slabs(counts_ref, index, counts_ref.shape[0])
    lines = tensor_ref[...].astype(F32).reshape(rows * slots, width).astype(BF16)
    at = lax.broadcasted_iota(I32, (rows * slots, rows * slots), 0)
    of = lax.broadcasted_iota(I32, (rows * slots, rows * slots), 1)
    pick = ((at % rows) * slots + at // rows == of).astype(F32).astype(BF16)
    by_slot = dot(pick, lines, NN)
    total = jnp.zeros((rows, sketch), F32)
    for slot in range(slots):
        slab = jnp.minimum(offset + slot, total_slabs - 1)
        picked = samples_ref[pl.ds(slab, 1), :]
        low = signs(32, picked & 31)
        high = signs(width // 32, picked >> 5)
        for part in range(width // 32):
            hadamard_ref[slot, pl.ds(part * 32, 32), :] = (low * high[part : part + 1, :]).astype(BF16)
        piece = by_slot[slot * rows : (slot + 1) * rows]
        scaled = (piece * scale_ref[pl.ds(slab, 1), :]).astype(BF16)
        term = dot(scaled, hadamard_ref[slot], NN)
        total = total + jnp.where(slot < count, term, 0.0)
    total_ref[...] = total * (1.0 / (total_slabs * width) ** 0.5)
    core = index % 2
    half = rows // 2
    keep_ref[...] = total_ref[pl.ds(pl.multiple_of(core * half, half), half), :]
    send_ref[...] = total_ref[pl.ds(pl.multiple_of((1 - core) * half, half), half), :]
    chunk = 128 // slots
    for chunk_index in range(width // chunk):
        start = chunk_index * chunk
        moved_ref[chunk_index] = jnp.concatenate(
            [by_slot[s * rows : (s + 1) * rows, start : start + chunk] for s in range(slots)], axis=1
        ).astype(BF16)


def sketch_parts(tensor, counts, scale, samples):
    rows, slots, width = tensor.shape
    sketch = samples.shape[1]
    chunks = width * slots // 128
    vmem = pl.BlockSpec(memory_space=pltpu.VMEM)
    half = jax.ShapeDtypeStruct((rows // 2, sketch), F32)
    return pl.pallas_call(
        sketch_kernel,
        out_shape=(half, half, jax.ShapeDtypeStruct((chunks, rows, 128), BF16)),
        in_specs=[vmem, pl.BlockSpec(memory_space=pltpu.SMEM), vmem, vmem],
        out_specs=(vmem, vmem, vmem),
        scratch_shapes=[pltpu.VMEM((slots, width, sketch), BF16), pltpu.VMEM((rows, sketch), F32)],
        name="sketch",
    )(tensor, counts, scale, samples)


def block_inverse(tiles):
    count = len(tiles)
    size = 8 * count
    lines = list(tiles)
    sub = lax.broadcasted_iota(I32, (8, 128), 0)
    lane = lax.broadcasted_iota(I32, (8, 128), 1)

    def row_of(tile, at):
        return jnp.broadcast_to(tile[at : at + 1, :], (8, 128))

    def column_of(tile, at):
        return jnp.broadcast_to(tile[:, at : at + 1], (8, 128))

    columns = {j: [column_of(tile, j) for tile in lines] for j in range(min(AHEAD, size))}
    pivots = [jnp.ones((8, 128), F32)] * count
    for step in range(size):
        tile, at = divmod(step, 8)
        column = columns.pop(step)
        pivot = row_of(column[tile], at)
        pivots[tile] = jnp.where(sub == at, pivot, pivots[tile])
        if step == size - 1:
            break
        inverse = 1.0 / pivot
        factors = {t: column[t] * inverse for t in range(tile, count)}
        factors[tile] = jnp.where(sub > at, factors[tile], 0.0)
        if at == 7:
            factors.pop(tile)
        for later in columns.values():
            value = row_of(later[tile], at)
            for t, factor in factors.items():
                later[t] = later[t] - factor * value
        line = jnp.where(lane == step, 1.0, row_of(lines[tile], at))
        for t, factor in factors.items():
            cleared = (lane == step) if t > tile else (lane == step) & (sub > at)
            lines[t] = jnp.where(cleared, 0.0, lines[t]) - factor * line
        new = step + AHEAD
        if new < size:
            columns[new] = [
                column_of(lines[t], new) if t >= (step + 1) // 8 else None for t in range(count)
            ]
    result = []
    for t in range(count):
        inside = jnp.where(lane == sub + 8 * t, 1.0, 0.0)
        result.append(lax.rsqrt(pivots[t]) * jnp.where(lane < sub + 8 * t, lines[t], inside))
    return jnp.concatenate(result, 0)


def factor_kernel(own_ref, other_ref, inverse_ref):
    size = own_ref.shape[1]
    inverse_ref[...] = dot(own_ref[...], own_ref[...], TN, HIGHEST) + dot(
        other_ref[...], other_ref[...], TN, HIGHEST
    )
    lanes = lax.broadcasted_iota(I32, (1, size), 1)

    def spread(block):
        return jnp.concatenate([block, jnp.zeros((BLOCK, 128 - BLOCK), F32)], 1)

    diagonal = spread(inverse_ref[0:BLOCK, 0:BLOCK])
    for start in range(0, size, BLOCK):
        end = start + BLOCK
        after = end + BLOCK
        inverse = block_inverse([diagonal[8 * t : 8 * t + 8] for t in range(BLOCK // 8)])[:, :BLOCK]
        if end < size:
            below = dot(inverse_ref[end:after, start:end], inverse, NT, HIGHEST)
            diagonal = spread(inverse_ref[end:after, end:after] - dot(below, below, NT, HIGHEST))
            rest = dot(inverse_ref[end:, start:end], inverse, NT, HIGHEST)
        inverse_ref[start:end, :] = dot(inverse, inverse_ref[start:end, :], NN, HIGHEST)
        inverse_ref[start:end, start:end] = inverse
        if end < size:
            here = (lanes >= start) & (lanes < end)
            inverse_ref[end:, :] = jnp.where(here, 0.0, inverse_ref[end:, :]) - dot(
                rest, inverse_ref[start:end, :], NN, HIGHEST
            )
    row = lax.broadcasted_iota(I32, (size, size), 0)
    column = lax.broadcasted_iota(I32, (size, size), 1)
    inverse_ref[...] = jnp.where(row >= column, inverse_ref[...], 0.0)


def inverse_factor(own, other):
    size = own.shape[1]
    vmem = pl.BlockSpec(memory_space=pltpu.VMEM)
    return pl.pallas_call(
        factor_kernel,
        out_shape=jax.ShapeDtypeStruct((size, size), F32),
        in_specs=[vmem, vmem],
        out_specs=vmem,
        name="factor",
    )(own, other)


def core_kernel(own_ref, other_ref, inverse_ref, moved_ref, counts_ref, basis_ref, core_ref, rows_ref):
    blocks, parts, line, size = rows_ref.shape
    index = lax.axis_index("yz")
    core = index % 2
    inverse = inverse_ref[...]
    for source, which in ((own_ref, core), (other_ref, 1 - core)):
        rows = dot(source[...], inverse, NT, HIGHEST).reshape(parts // 2, blocks, line, size)
        for part in range(parts // 2):
            rows_ref[:, which * (parts // 2) + part] = rows[part]
    basis_ref[...] = rows_ref[lax.axis_index("gx")].reshape(parts * line, size)
    every = rows_ref[...].reshape(blocks * parts * line, size).astype(BF16)
    moved = moved_ref[...].reshape(blocks * parts * line, 128)
    result = dot(moved, every, TN)
    slots = 4
    slot = lax.broadcasted_iota(I32, result.shape, 0) // (128 // slots)
    core_ref[...] = jnp.where(slot < counts_ref[index], result, 0.0).astype(BF16)


def core_and_basis(own, other, inverse, moved, counts):
    size = own.shape[1]
    blocks, rows, _ = moved.shape
    vmem = pl.BlockSpec(memory_space=pltpu.VMEM)
    return pl.pallas_call(
        core_kernel,
        out_shape=(
            jax.ShapeDtypeStruct((rows, size), F32),
            jax.ShapeDtypeStruct((128, size), BF16),
        ),
        in_specs=[vmem, vmem, vmem, vmem, pl.BlockSpec(memory_space=pltpu.SMEM)],
        out_specs=(vmem, vmem),
        scratch_shapes=[pltpu.VMEM((blocks, rows // 8, 8, size), F32)],
        name="core",
    )(own, other, inverse, moved, counts)


def local(tensor_slabs, slab_counts, column_scale, samples):
    rows, slots, width = tensor_slabs.shape
    sketch = samples.shape[1]
    blocks = lax.axis_size("gx")
    members = lax.axis_size("yz")
    chips = members // 2
    swap = [(j, j ^ 1) for j in range(members)]
    same_core = [[2 * y + c for y in range(chips)] for c in range(2)]
    keep, send, chunks = sketch_parts(tensor_slabs, slab_counts, column_scale, samples)
    half = keep + lax.ppermute(send, "yz", swap)
    parts = lax.all_to_all(
        half.reshape(chips, -1, sketch), "yz", 0, 0, axis_index_groups=same_core, tiled=True
    )
    part = parts.sum(0)
    column = lax.all_to_all(jnp.broadcast_to(part, (blocks, *part.shape)), "gx", 0, 0, tiled=True)
    column = column.reshape(-1, sketch)
    own = lax.all_to_all(
        jnp.broadcast_to(column, (chips, *column.shape)), "yz", 0, 0,
        axis_index_groups=same_core, tiled=True,
    ).reshape(-1, sketch)
    other = lax.ppermute(own, "yz", swap)
    own, other, chunks = lax.optimization_barrier((own, other, chunks))
    moved = lax.all_to_all(chunks, "gx", 0, 0, tiled=True)
    inverse = inverse_factor(own, other)
    basis, core = core_and_basis(own, other, inverse, moved, slab_counts)
    core = jnp.moveaxis(core.reshape(slots, -1, sketch), 2, 0)
    return basis, core


def solution(mesh):
    placed = (P("gx", "yz", None), P(), P(), P())
    return jax.shard_map(
        local,
        mesh=mesh,
        in_specs=placed,
        out_specs=(P("gx", None), P(None, "yz", "gx")),
        check_vma=False,
    )
```

time: 179 us -> 84.6 us (0.47)
  other arithmetic: 61.8 us -> 0.77 us
  waiting for transfers between devices: 30.8 us -> 8.08 us
  Pallas kernels: 0 us -> 20.8 us
  starting transfers between devices: 21.2 us -> 6.42 us
  local copies, waits for them, and re-layouts: 12.3 us -> 0.91 us
  blocking collectives: 36.8 us -> 46.5 us
  matrix products: 8.79 us -> 0 us
  between operations: 3.94 us -> 0.67 us
  loops' own time: 2.63 us -> 0 us
    another operation x9 -> x0, other arithmetic: 53.9 us -> none  [the longest x6 33.9 us: local(): cholesky_factor = jnp.linalg.cholesky(gram_matrix)]
    all_to_all x3 -> x1, waiting for transfers between devices: 30.8 us -> 4.01 us  [local(): moved = lax.all_to_all(chunks, 'gx', 0, 0, tiled=True)]
    pallas_call x0 -> x3, Pallas kernels: none -> 20.8 us  [the longest x1 13.1 us: inverse_factor(): pl.pallas_call(factor_kernel, out_shape=jax.ShapeDtypeStruct((size, size)...]
    all_to_all x3 -> x1, starting transfers between devices: 21.2 us -> 6.41 us  [local(): moved = lax.all_to_all(chunks, 'gx', 0, 0, tiled=True)]
    all_to_all x2 -> x3, blocking collectives: 36.8 us -> 46.5 us  [the longest x1 21.5 us: local(): lax.all_to_all(jnp.broadcast_to(part, (blocks, *part.shape)), 'gx', 0, 0,...]
    dot_general x6 -> x0, matrix products: 7.71 us -> none  [the longest x4 6.37 us: add_slab(): jnp.dot(scaled, hadamard_part, preferred_element_type=jnp.float32)]
    convert_element_type x6 -> x0, other arithmetic: 6.36 us -> none  [the longest x4 5.15 us: add_slab(): piece.astype(jnp.float32) * slab_scale[None, :]]
    ppermute x0 -> x2, waiting for transfers between devices: none -> 4.07 us  [the longest x1 2.66 us: local(): other = lax.ppermute(own, 'yz', swap)]
  transfers between devices with their start and end apart: 3 -> 3, of which waited for: 2 -> 3; matrix products, arithmetic and copies ran while one was open for 36% -> 0% of each run, Pallas kernels for 0% -> 16%
where the time goes in v1:
time: 84.6 us; the launch traced here: 84.1 us
  blocking collectives  46.5 us (55%)
  Pallas kernels  20.8 us (25%)
  waiting for transfers between devices  8.08 us (10%)
  starting transfers between devices  6.42 us (8%)
  local copies, waits for them, and re-layouts  0.91 us (1%)
    all_to_all x1, blocking collectives, local(): lax.all_to_all(jnp.broadcast_to(part, (blocks, *part.shape)), 'gx', 0, 0,...  21.5 us
    all_to_all x1, blocking collectives, local(): lax.all_to_all(jnp.broadcast_to(column, (chips, *column.shape)), 'yz', 0,...  15.2 us
    pallas_call x1, Pallas kernels, inverse_factor(): pl.pallas_call(factor_kernel, out_shape=jax.ShapeDtypeStruct((size, size)...  13.1 us
    all_to_all x1, blocking collectives, local(): lax.all_to_all(half.reshape(chips, -1, sketch), 'yz', 0, 0, axis_index_gr...  9.7 us
    all_to_all x1, starting transfers between devices, local(): moved = lax.all_to_all(chunks, 'gx', 0, 0, tiled=True)  6.41 us
    pallas_call x1, Pallas kernels, core_and_basis(): pl.pallas_call(core_kernel, out_shape=(jax.ShapeDtypeStruct((rows, size),...  4.86 us
    all_to_all x1, waiting for transfers between devices, local(): moved = lax.all_to_all(chunks, 'gx', 0, 0, tiled=True)  4.01 us
    pallas_call x1, Pallas kernels, sketch_parts(): pl.pallas_call(sketch_kernel, out_shape=(half, half, jax.ShapeDtypeStruct...  2.88 us
  transfers between devices with their start and end apart: 3, of which 3 were waited for; matrix products, arithmetic and copies ran while one was open for 0% of the time, Pallas kernels for 16%

profile of v1, /device:TPU:2, one launch (start us, length us, event | category | flops | bytes accessed | tf_op | source)
XLA Modules:
  0.0 84.1 jit_solution(6229780841425588362)
XLA Ops:
  0.6 2.9 %sketch.1 = (f32[32,256]{1,0:T(8,128)}, f32[32,256]{1,0:T(8,128)}, bf16[32,64,128]{2,1,0:T(8,128)(2,1)}) custom-call(bf16[64,4,1024]{2,1,0:T(4,128)(2,1)} %tensor_ref.1, s32[8]{0:T(128)} %counts_ref.3, f32[16,1024]{1,0:T(8,128)} %scale_ref.1, s32[16,256]{1,0:T(8,128)} %samples_ref.1), custom_call_target="tpu_custom_call" | custom-call | tf_op jit(solution)/shard_map/sketch/pallas_call | solution.py:80
  3.5 0.0 collective-permute-start
  3.5 1.4 %collective-permute-done = f32[32,256]{1,0:T(8,128)S(1)} collective-permute-done((f32[32,256]{1,0:T(8,128)}, f32[32,256]{1,0:T(8,128)S(1)}, u32[]{:S(2)}, u32[]{:S(2)}) %collective-permute-start) | collective-permute-done | bytes 32800 | tf_op jit(solution)/shard_map/ppermute | solution.py:224
  4.9 0.8 add_bitcast_fusion
  5.7 9.7 %all_to_all.20 = f32[4,8,256]{2,1,0:T(8,128)S(1)} all-to-all(f32[4,8,256]{2,1,0:T(8,128)S(1)} %add_bitcast_fusion), channel_id=1, replica_groups={{0,2,4,6},{1,3,5,7},{8,10,12,14},{9,11,13,15},{16,18,20,22},{17,19,21,2..., dimensions={0} | all-to-all | bytes 65536 | tf_op jit(solution)/shard_map/all_to_all | solution.py:225
  15.4 21.5 %all_to_all.21 = f32[32,8,256]{2,1,0:T(8,128)S(1)} all-to-all(f32[32,8,256]{2,1,0:T(8,128)S(1)} %broadcast_in_dim.6), channel_id=1, replica_groups=mesh['gx'=32,'yz'=8] {'gx'}, dimensions={0} | all-to-all | bytes 524288 | tf_op jit(solution)/shard_map/all_to_all | solution.py:229
  37.0 0.1 broadcast_in_dim.7
  37.0 15.2 %all_to_all.22 = f32[4,256,256]{2,1,0:T(8,128)S(1)} all-to-all(f32[4,256,256]{2,1,0:T(8,128)S(1)} %broadcast_in_dim.7), channel_id=1, replica_groups={{0,2,4,6},{1,3,5,7},{8,10,12,14},{9,11,13,15},{16,18,20,22},{17,19,21,2..., dimensions={0} | all-to-all | bytes 2097152 | tf_op jit(solution)/shard_map/all_to_all | solution.py:231
  52.3 0.0 copy-start
  52.3 0.0 collective-permute-start.1
  52.3 2.7 %collective-permute-done.1.other_ref = f32[1024,256]{1,0:T(8,128)S(1)} collective-permute-done((f32[1024,256]{1,0:T(8,128)S(1)}, f32[1024,256]{1,0:T(8,128)S(1)}, u32[]{:S(2)}, u32[]{:S(2)}) %collective-permute-start.1) | collective-permute-done | bytes 1048608 | tf_op jit(solution)/shard_map/ppermute | solution.py:235
  54.9 0.0 copy-start.1
  54.9 6.4 %all-to-all-start.3 = ((bf16[32,64,128]{2,1,0:T(8,128)(2,1)}), bf16[32,64,128]{2,1,0:T(8,128)(2,1)S(1)}, u32[]{:S(2)}, u32[]{:S(2)}) async-start(bf16[32,64,128]{2,1,0:T(8,128)(2,1)} %get-tuple-element.15), calls=%async_computation.3 | async-start | bytes 1048576 | tf_op jit(solution)/shard_map/all_to_all | solution.py:237
  61.4 0.0 copy-done
  61.4 0.0 copy-done.1
  61.4 13.1 %factor.1.inverse_ref = f32[256,256]{1,0:T(8,128)} custom-call(f32[1024,256]{1,0:T(8,128)} %bitcast.8, f32[1024,256]{1,0:T(8,128)} %copy-done.1), custom_call_target="tpu_custom_call" | custom-call | tf_op jit(solution)/shard_map/factor/pallas_call | solution.py:171
  74.5 4.0 %all-to-all-done.3.moved_ref = bf16[32,64,128]{2,1,0:T(8,128)(2,1)S(1)} async-done(((bf16[32,64,128]{2,1,0:T(8,128)(2,1)}), bf16[32,64,128]{2,1,0:T(8,128)(2,1)S(1)}, u32[]{:S(2)}, u32[]{:S(2)}) %all-to-all-start.3) | async-done | bytes 524320 | tf_op jit(solution)/shard_map/all_to_all | solution.py:237
  78.5 0.0 copy-start.2
  78.5 0.8 copy-done.2
  79.3 4.9 %core.1 = (f32[64,256]{1,0:T(8,128)}, bf16[128,256]{1,0:T(8,128)(2,1)}) custom-call(f32[1024,256]{1,0:T(8,128)} %bitcast.9, f32[1024,256]{1,0:T(8,128)} %copy-done.1, f32[256,256]{1,0:T(8,128)} %factor.1.inverse_ref, bf16[32,64,128]{2,1,0:T(8,128)(2,1)} %copy-done.2, s32[8]{0:T(128)} %counts_ref.3), custom_call_target="tpu_custom_call" | custom-call | tf_op jit(solution)/shard_map/core/pallas_call | solution.py:202
  (2 shorter events, 0.0 us)
Async XLA Ops:
  3.5 1.4 %collective-permute-start = (f32[32,256]{1,0:T(8,128)}, f32[32,256]{1,0:T(8,128)S(1)}, u32[]{:S(2)}, u32[]{:S(2)}) collective-permute-start(f32[32,256]{1,0:T(8,128)} %get-tuple-element.11), channel_id=1, source_target_pairs={{0,1},{1,0},{2,3},{3,2},{4,5},{5,4},{6,7},{7,6},{8,9},{9,8},{10,11... | collective-permute-start | bytes 98312 | tf_op jit(solution)/shard_map/ppermute | solution.py:224
  52.3 9.1 %copy-start = (f32[4,256,256]{2,1,0:T(8,128)}, f32[4,256,256]{2,1,0:T(8,128)S(1)}, u32[]{:S(2)}) copy-start(f32[4,256,256]{2,1,0:T(8,128)S(1)} %all_to_all.22) | copy-start | bytes 3145732
  52.3 2.7 %collective-permute-start.1 = (f32[1024,256]{1,0:T(8,128)S(1)}, f32[1024,256]{1,0:T(8,128)S(1)}, u32[]{:S(2)}, u32[]{:S(2)}) collective-permute-start(f32[1024,256]{1,0:T(8,128)S(1)} %bitcast.7), channel_id=1, source_target_pairs={{0,1},{1,0},{2,3},{3,2},{4,5},{5,4},{6,7},{7,6},{8,9},{9,8},{10,11... | collective-permute-start | bytes 3145736 | tf_op jit(solution)/shard_map/ppermute | solution.py:235
  54.9 6.4 %copy-start.1 = (f32[1024,256]{1,0:T(8,128)}, f32[1024,256]{1,0:T(8,128)S(1)}, u32[]{:S(2)}) copy-start(f32[1024,256]{1,0:T(8,128)S(1)} %collective-permute-done.1.other_ref) | copy-start | bytes 3145732
  54.9 23.5 %all-to-all-start.3 = ((bf16[32,64,128]{2,1,0:T(8,128)(2,1)}), bf16[32,64,128]{2,1,0:T(8,128)(2,1)S(1)}, u32[]{:S(2)}, u32[]{:S(2)}) async-start(bf16[32,64,128]{2,1,0:T(8,128)(2,1)} %get-tuple-element.15), calls=%async_computation.3 | async-start | bytes 1048576 | tf_op jit(solution)/shard_map/all_to_all | solution.py:237
  78.5 0.8 copy-start.2

commit v2 on v1

--- a/solution.py
+++ b/solution.py
@@ -1,5 +1,3 @@
-import functools
-
 import jax
 import jax.numpy as jnp
 from jax import lax
@@ -7,11 +5,13 @@
 from jax.experimental.pallas import tpu as pltpu
 from jax.sharding import PartitionSpec as P
 
+
 F32, BF16, I32 = jnp.float32, jnp.bfloat16, jnp.int32
 NN, NT, TN = ((1,), (0,)), ((1,), (1,)), ((0,), (0,))
 HIGHEST = lax.Precision.HIGHEST
 AHEAD = 10
 BLOCK = 64
+STEPS = (0, 2, 1, 3)
 
 
 def dot(a, b, dims, precision=None):
@@ -134,86 +134,98 @@
     return jnp.concatenate(result, 0)
 
 
-def factor_kernel(own_ref, other_ref, inverse_ref):
-    size = own_ref.shape[1]
-    inverse_ref[...] = dot(own_ref[...], own_ref[...], TN, HIGHEST) + dot(
-        other_ref[...], other_ref[...], TN, HIGHEST
-    )
+def invert_factor(work_ref):
+    size = work_ref.shape[0]
     lanes = lax.broadcasted_iota(I32, (1, size), 1)
 
     def spread(block):
         return jnp.concatenate([block, jnp.zeros((BLOCK, 128 - BLOCK), F32)], 1)
 
-    diagonal = spread(inverse_ref[0:BLOCK, 0:BLOCK])
+    diagonal = spread(work_ref[0:BLOCK, 0:BLOCK])
     for start in range(0, size, BLOCK):
         end = start + BLOCK
         after = end + BLOCK
         inverse = block_inverse([diagonal[8 * t : 8 * t + 8] for t in range(BLOCK // 8)])[:, :BLOCK]
         if end < size:
-            below = dot(inverse_ref[end:after, start:end], inverse, NT, HIGHEST)
-            diagonal = spread(inverse_ref[end:after, end:after] - dot(below, below, NT, HIGHEST))
-            rest = dot(inverse_ref[end:, start:end], inverse, NT, HIGHEST)
-        inverse_ref[start:end, :] = dot(inverse, inverse_ref[start:end, :], NN, HIGHEST)
-        inverse_ref[start:end, start:end] = inverse
+            below = dot(work_ref[end:after, start:end], inverse, NT, HIGHEST)
+            diagonal = spread(work_ref[end:after, end:after] - dot(below, below, NT, HIGHEST))
+            rest = dot(work_ref[end:, start:end], inverse, NT, HIGHEST)
+        work_ref[start:end, :] = dot(inverse, work_ref[start:end, :], NN, HIGHEST)
+        work_ref[start:end, start:end] = inverse
         if end < size:
             here = (lanes >= start) & (lanes < end)
-            inverse_ref[end:, :] = jnp.where(here, 0.0, inverse_ref[end:, :]) - dot(
-                rest, inverse_ref[start:end, :], NN, HIGHEST
+            work_ref[end:, :] = jnp.where(here, 0.0, work_ref[end:, :]) - dot(
+                rest, work_ref[start:end, :], NN, HIGHEST
             )
     row = lax.broadcasted_iota(I32, (size, size), 0)
     column = lax.broadcasted_iota(I32, (size, size), 1)
-    inverse_ref[...] = jnp.where(row >= column, inverse_ref[...], 0.0)
-
-
-def inverse_factor(own, other):
-    size = own.shape[1]
-    vmem = pl.BlockSpec(memory_space=pltpu.VMEM)
-    return pl.pallas_call(
-        factor_kernel,
-        out_shape=jax.ShapeDtypeStruct((size, size), F32),
-        in_specs=[vmem, vmem],
-        out_specs=vmem,
-        name="factor",
-    )(own, other)
-
-
-def core_kernel(own_ref, other_ref, inverse_ref, moved_ref, counts_ref, basis_ref, core_ref, rows_ref):
+    work_ref[...] = jnp.where(row >= column, work_ref[...], 0.0)
+
+
+def halves(array):
+    high = array.astype(BF16)
+    return high, (array - high.astype(F32)).astype(BF16)
+
+
+def finish_kernel(*refs):
+    sources, (counts_ref, basis_ref, core_ref), scratch = refs[:9], refs[9:12], refs[12:]
+    work_ref, rows_ref, sems = scratch
     blocks, parts, line, size = rows_ref.shape
+    chips = parts // 2
     index = lax.axis_index("yz")
-    core = index % 2
-    inverse = inverse_ref[...]
-    for source, which in ((own_ref, core), (other_ref, 1 - core)):
-        rows = dot(source[...], inverse, NT, HIGHEST).reshape(parts // 2, blocks, line, size)
-        for part in range(parts // 2):
-            rows_ref[:, which * (parts // 2) + part] = rows[part]
-    basis_ref[...] = rows_ref[lax.axis_index("gx")].reshape(parts * line, size)
-    every = rows_ref[...].reshape(blocks * parts * line, size).astype(BF16)
-    moved = moved_ref[...].reshape(blocks * parts * line, 128)
-    result = dot(moved, every, TN)
+    core, chip = index % 2, index // 2
+    places = [
+        which * chips + (chip + chips - step) % chips for which in (core, 1 - core) for step in STEPS
+    ]
+    copies = [
+        pltpu.make_async_copy(source, rows_ref.at[:, place], sems.at[number])
+        for number, (source, place) in enumerate(zip(sources[:8], places))
+    ]
+    for copy in copies:
+        copy.start()
+    gram = jnp.zeros((size, size), F32)
+    for source in sources[:8]:
+        piece = source[...].reshape(blocks * line, size)
+        gram = gram + dot(piece, piece, TN, HIGHEST)
+    work_ref[...] = gram
+    invert_factor(work_ref)
+    for copy in copies:
+        copy.wait()
+    inverse = work_ref[...]
+    inverse_high, inverse_low = halves(inverse)
+    block = rows_ref[lax.axis_index("gx")].reshape(parts * line, size)
+    basis_ref[...] = dot(block, inverse, NT, HIGHEST)
+    high, low = halves(rows_ref[...].reshape(blocks * parts * line, size))
+    every = dot(high, inverse_high, NT) + dot(high, inverse_low, NT) + dot(low, inverse_high, NT)
+    result = dot(sources[8][...].reshape(blocks * parts * line, 128), every.astype(BF16), TN)
     slots = 4
     slot = lax.broadcasted_iota(I32, result.shape, 0) // (128 // slots)
     core_ref[...] = jnp.where(slot < counts_ref[index], result, 0.0).astype(BF16)
 
 
-def core_and_basis(own, other, inverse, moved, counts):
-    size = own.shape[1]
+def finish(pieces, moved, counts):
     blocks, rows, _ = moved.shape
+    line, size = pieces[0].shape[1:]
     vmem = pl.BlockSpec(memory_space=pltpu.VMEM)
     return pl.pallas_call(
-        core_kernel,
+        finish_kernel,
         out_shape=(
             jax.ShapeDtypeStruct((rows, size), F32),
             jax.ShapeDtypeStruct((128, size), BF16),
         ),
-        in_specs=[vmem, vmem, vmem, vmem, pl.BlockSpec(memory_space=pltpu.SMEM)],
+        in_specs=[vmem] * 9 + [pl.BlockSpec(memory_space=pltpu.SMEM)],
         out_specs=(vmem, vmem),
-        scratch_shapes=[pltpu.VMEM((blocks, rows // 8, 8, size), F32)],
-        name="core",
-    )(own, other, inverse, moved, counts)
+        scratch_shapes=[
+            pltpu.VMEM((size, size), F32),
+            pltpu.VMEM((blocks, rows // line, line, size), F32),
+            pltpu.SemaphoreType.DMA((8,)),
+        ],
+        name="finish",
+    )(*(pltpu.with_memory_space_constraint(each, pltpu.VMEM) for each in (*pieces, moved)), counts)
 
 
 def local(tensor_slabs, slab_counts, column_scale, samples):
-    rows, slots, width = tensor_slabs.shape
+    _, slots, _ = tensor_slabs.shape
     sketch = samples.shape[1]
     blocks = lax.axis_size("gx")
     members = lax.axis_size("yz")
@@ -225,18 +237,16 @@
     parts = lax.all_to_all(
         half.reshape(chips, -1, sketch), "yz", 0, 0, axis_index_groups=same_core, tiled=True
     )
-    part = parts.sum(0)
-    column = lax.all_to_all(jnp.broadcast_to(part, (blocks, *part.shape)), "gx", 0, 0, tiled=True)
-    column = column.reshape(-1, sketch)
-    own = lax.all_to_all(
-        jnp.broadcast_to(column, (chips, *column.shape)), "yz", 0, 0,
-        axis_index_groups=same_core, tiled=True,
-    ).reshape(-1, sketch)
-    other = lax.ppermute(own, "yz", swap)
-    own, other, chunks = lax.optimization_barrier((own, other, chunks))
+    part = jnp.broadcast_to(parts.sum(0), (blocks, *parts.shape[1:]))
+    column = lax.all_to_all(part, "gx", 0, 0, tiled=True)
+    pieces = [column]
+    for step in STEPS[1:]:
+        turn = [(j, (j + 2 * step) % members) for j in range(members)]
+        pieces.append(lax.ppermute(column, "yz", turn))
     moved = lax.all_to_all(chunks, "gx", 0, 0, tiled=True)
-    inverse = inverse_factor(own, other)
-    basis, core = core_and_basis(own, other, inverse, moved, slab_counts)
+    live = jnp.minimum(slab_counts, slots)
+    pieces = pieces + [lax.ppermute(piece, "yz", swap) for piece in pieces]
+    basis, core = finish(pieces, moved, live)
     core = jnp.moveaxis(core.reshape(slots, -1, sketch), 2, 0)
     return basis, core
 

time: 84.6 us -> 74.7 us (0.88); the launches traced: 84.1 us -> 73.2 us
  blocking collectives: 46.5 us -> 31.2 us
  waiting for transfers between devices: 8.08 us -> 11.9 us
  starting transfers between devices: 6.42 us -> 9.9 us
  Pallas kernels: 20.8 us -> 18.1 us
  local copies, waits for them, and re-layouts: 0.91 us -> 0.03 us
    all_to_all x2 -> x1, blocking collectives: 36.8 us -> 21.5 us  [local(): column = lax.all_to_all(part, 'gx', 0, 0, tiled=True)]
    ppermute x1 -> x7, waiting for transfers between devices: 2.66 us -> 10.3 us  [the longest x3 9.62 us: local(): pieces.append(lax.ppermute(column, 'yz', turn))]
    ppermute x1 -> x7, starting transfers between devices: 0.01 us -> 4 us  [the longest x3 3.48 us: local(): pieces.append(lax.ppermute(column, 'yz', turn))]
    all_to_all x1, waiting for transfers between devices: 4.01 us -> 0.19 us  [local(): moved = lax.all_to_all(chunks, 'gx', 0, 0, tiled=True)]
    pallas_call x2 -> x1, Pallas kernels: 18 us -> 15.2 us  [finish(): pl.pallas_call(finish_kernel, out_shape=(jax.ShapeDtypeStruct((rows, size...]
  transfers between devices with their start and end apart: 3 -> 9, of which waited for: 3 -> 6; matrix products, arithmetic and copies ran while one was open for 0% -> 1% of each run, Pallas kernels for 16% -> 0%
where the time goes in v2:
time: 74.7 us; the launch traced here: 73.2 us
  blocking collectives  31.2 us (42%)
  Pallas kernels  18.1 us (24%)
  waiting for transfers between devices  11.9 us (16%)
  starting transfers between devices  9.9 us (13%)
  other arithmetic  1.29 us (2%)
  between operations  0.82 us (1%)
    all_to_all x1, blocking collectives, local(): column = lax.all_to_all(part, 'gx', 0, 0, tiled=True)  21.5 us
    pallas_call x1, Pallas kernels, finish(): pl.pallas_call(finish_kernel, out_shape=(jax.ShapeDtypeStruct((rows, size...  15.2 us
    all_to_all x1, blocking collectives, local(): lax.all_to_all(half.reshape(chips, -1, sketch), 'yz', 0, 0, axis_index_gr...  9.7 us
    ppermute x3, waiting for transfers between devices, local(): pieces.append(lax.ppermute(column, 'yz', turn))  9.62 us
    all_to_all x1, starting transfers between devices, local(): moved = lax.all_to_all(chunks, 'gx', 0, 0, tiled=True)  5.9 us
    ppermute x3, starting transfers between devices, local(): pieces.append(lax.ppermute(column, 'yz', turn))  3.48 us
    pallas_call x1, Pallas kernels, sketch_parts(): pl.pallas_call(sketch_kernel, out_shape=(half, half, jax.ShapeDtypeStruct...  2.87 us
  transfers between devices with their start and end apart: 9, of which 6 were waited for; matrix products, arithmetic and copies ran while one was open for 1% of the time, Pallas kernels for 0%

profile of v2, /device:TPU:2, one launch (start us, length us, event | category | flops | bytes accessed | tf_op | source)
XLA Modules:
  0.0 73.2 jit_solution(16379475747789612137)
XLA Ops:
  0.6 2.9 %sketch.1 = (f32[32,256]{1,0:T(8,128)}, f32[32,256]{1,0:T(8,128)}, bf16[32,64,128]{2,1,0:T(8,128)(2,1)}) custom-call(bf16[64,4,1024]{2,1,0:T(4,128)(2,1)} %tensor_ref.1, s32[8]{0:T(128)} %counts_ref.1, f32[16,1024]{1,0:T(8,128)} %scale_ref.1, s32[16,256]{1,0:T(8,128)} %samples_ref.1), custom_call_target="tpu_custom_call" | custom-call | tf_op jit(solution)/shard_map/sketch/pallas_call | solution.py:80
  3.5 0.0 collective-permute-start
  3.5 1.4 %collective-permute-done = f32[32,256]{1,0:T(8,128)S(1)} collective-permute-done((f32[32,256]{1,0:T(8,128)}, f32[32,256]{1,0:T(8,128)S(1)}, u32[]{:S(2)}, u32[]{:S(2)}) %collective-permute-start) | collective-permute-done | bytes 32800 | tf_op jit(solution)/shard_map/ppermute | solution.py:236
  4.9 0.8 %add_bitcast_fusion = f32[4,8,256]{2,1,0:T(8,128)S(1)} fusion(f32[32,256]{1,0:T(8,128)} %get-tuple-element.7, f32[32,256]{1,0:T(8,128)S(1)} %collective-permute-done), kind=kLoop, calls=%fused_computation | loop fusion | flops 8192 | bytes 98304 | tf_op jit(solution)/shard_map/reshape | solution.py:238
  5.7 9.7 %all_to_all.15 = f32[4,8,256]{2,1,0:T(8,128)S(1)} all-to-all(f32[4,8,256]{2,1,0:T(8,128)S(1)} %add_bitcast_fusion), channel_id=1, replica_groups={{0,2,4,6},{1,3,5,7},{8,10,12,14},{9,11,13,15},{16,18,20,22},{17,19,21,2..., dimensions={0} | all-to-all | bytes 65536 | tf_op jit(solution)/shard_map/all_to_all | solution.py:237
  15.4 21.5 %all_to_all.16.refs_0_ = f32[32,8,256]{2,1,0:T(8,128)S(1)} all-to-all(f32[32,8,256]{2,1,0:T(8,128)S(1)} %broadcast_in_dim.3), channel_id=1, replica_groups=mesh['gx'=32,'yz'=8] {'gx'}, dimensions={0} | all-to-all | bytes 524288 | tf_op jit(solution)/shard_map/all_to_all | solution.py:241
  36.9 0.0 copy-start
  36.9 5.9 %all-to-all-start.2 = ((bf16[32,64,128]{2,1,0:T(8,128)(2,1)}), bf16[32,64,128]{2,1,0:T(8,128)(2,1)S(1)}, u32[]{:S(2)}, u32[]{:S(2)}) async-start(bf16[32,64,128]{2,1,0:T(8,128)(2,1)} %get-tuple-element.9), calls=%async_computation.2 | async-start | bytes 1048576 | tf_op jit(solution)/shard_map/all_to_all | solution.py:246
  42.9 1.2 %collective-permute-start.3 = (f32[32,8,256]{2,1,0:T(8,128)S(1)}, f32[32,8,256]{2,1,0:T(8,128)S(1)}, u32[]{:S(2)}, u32[]{:S(2)}) collective-permute-start(f32[32,8,256]{2,1,0:T(8,128)S(1)} %all_to_all.16.refs_0_), channel_id=1, source_target_pairs={{0,6},{1,7},{2,0},{3,1},{4,2},{5,3},{6,4},{7,5},{8,14},{9,15},{10,... | collective-permute-start | bytes 786440 | tf_op jit(solution)/shard_map/ppermute | solution.py:245
  44.1 0.9 %collective-permute-start.2 = (f32[32,8,256]{2,1,0:T(8,128)S(1)}, f32[32,8,256]{2,1,0:T(8,128)S(1)}, u32[]{:S(2)}, u32[]{:S(2)}) collective-permute-start(f32[32,8,256]{2,1,0:T(8,128)S(1)} %all_to_all.16.refs_0_), channel_id=1, source_target_pairs={{0,2},{1,3},{2,4},{3,5},{4,6},{5,7},{6,0},{7,1},{8,10},{9,11},{10,... | collective-permute-start | bytes 786440 | tf_op jit(solution)/shard_map/ppermute | solution.py:245
  45.0 1.4 %collective-permute-start.1 = (f32[32,8,256]{2,1,0:T(8,128)S(1)}, f32[32,8,256]{2,1,0:T(8,128)S(1)}, u32[]{:S(2)}, u32[]{:S(2)}) collective-permute-start(f32[32,8,256]{2,1,0:T(8,128)S(1)} %all_to_all.16.refs_0_), channel_id=1, source_target_pairs={{0,4},{1,5},{2,6},{3,7},{4,0},{5,1},{6,2},{7,3},{8,12},{9,13},{10,... | collective-permute-start | bytes 786440 | tf_op jit(solution)/shard_map/ppermute | solution.py:245
  46.3 0.0 collective-permute-start.4
  46.3 4.4 %collective-permute-done.3.refs_3_ = f32[32,8,256]{2,1,0:T(8,128)S(1)} collective-permute-done((f32[32,8,256]{2,1,0:T(8,128)S(1)}, f32[32,8,256]{2,1,0:T(8,128)S(1)}, u32[]{:S(2)}, u32[]{:S(2)}) %collective-permute-start.3) | collective-permute-done | bytes 262176 | tf_op jit(solution)/shard_map/ppermute | solution.py:245
  50.7 0.0 collective-permute-start.7
  50.7 5.2 %collective-permute-done.2.refs_2_ = f32[32,8,256]{2,1,0:T(8,128)S(1)} collective-permute-done((f32[32,8,256]{2,1,0:T(8,128)S(1)}, f32[32,8,256]{2,1,0:T(8,128)S(1)}, u32[]{:S(2)}, u32[]{:S(2)}) %collective-permute-start.2) | collective-permute-done | bytes 262176 | tf_op jit(solution)/shard_map/ppermute | solution.py:245
  56.0 0.0 collective-permute-start.6
  56.0 0.0 collective-permute-done.1.refs_1_
  56.0 0.5 collective-permute-start.5
  56.5 0.0 copy-done
  56.5 0.5 broadcast_minimum_fusion.refs_9_
  57.0 0.0 collective-permute-done.4.refs_4_
  57.0 0.2 all-to-all-done.2.refs_8_
  57.2 0.0 collective-permute-done.7.refs_7_
  57.2 0.3 collective-permute-done.6.refs_6_
  57.5 0.4 collective-permute-done.5.refs_5_
  57.9 15.2 %finish.1 = (f32[64,256]{1,0:T(8,128)}, bf16[128,256]{1,0:T(8,128)(2,1)}) custom-call(f32[32,8,256]{2,1,0:T(8,128)S(1)} %all_to_all.16.refs_0_, f32[32,8,256]{2,1,0:T(8,128)S(1)} %collective-permute-done.1.refs_1_, f32[32,8,256]{2,1,0:T(8,128)S(1)} %collective-permute-done.2.refs_2_, f32[32,8,256]{2,1,0:T(8,128)S(1)} %collective-permute-done.3.refs_3_, ...), custom_call_target="tpu_custom_call" | custom-call | tf_op jit(solution)/shard_map/finish/pallas_call | solution.py:210
  (2 shorter events, 0.0 us)
Async XLA Ops:
  3.5 1.4 %collective-permute-start = (f32[32,256]{1,0:T(8,128)}, f32[32,256]{1,0:T(8,128)S(1)}, u32[]{:S(2)}, u32[]{:S(2)}) collective-permute-start(f32[32,256]{1,0:T(8,128)} %get-tuple-element.8), channel_id=1, source_target_pairs={{0,1},{1,0},{2,3},{3,2},{4,5},{5,4},{6,7},{7,6},{8,9},{9,8},{10,11... | collective-permute-start | bytes 98312 | tf_op jit(solution)/shard_map/ppermute | solution.py:236
  36.9 19.5 %copy-start = (s32[8]{0:T(128)S(1)}, s32[8]{0:T(128)}, u32[]{:S(2)}) copy-start(s32[8]{0:T(128)} %counts_ref.1) | copy-start | bytes 100
  36.9 20.3 %all-to-all-start.2 = ((bf16[32,64,128]{2,1,0:T(8,128)(2,1)}), bf16[32,64,128]{2,1,0:T(8,128)(2,1)S(1)}, u32[]{:S(2)}, u32[]{:S(2)}) async-start(bf16[32,64,128]{2,1,0:T(8,128)(2,1)} %get-tuple-element.9), calls=%async_computation.2 | async-start | bytes 1048576 | tf_op jit(solution)/shard_map/all_to_all | solution.py:246
  42.9 7.9 %collective-permute-start.3 = (f32[32,8,256]{2,1,0:T(8,128)S(1)}, f32[32,8,256]{2,1,0:T(8,128)S(1)}, u32[]{:S(2)}, u32[]{:S(2)}) collective-permute-start(f32[32,8,256]{2,1,0:T(8,128)S(1)} %all_to_all.16.refs_0_), channel_id=1, source_target_pairs={{0,6},{1,7},{2,0},{3,1},{4,2},{5,3},{6,4},{7,5},{8,14},{9,15},{10,... | collective-permute-start | bytes 786440 | tf_op jit(solution)/shard_map/ppermute | solution.py:245
  44.1 11.9 %collective-permute-start.2 = (f32[32,8,256]{2,1,0:T(8,128)S(1)}, f32[32,8,256]{2,1,0:T(8,128)S(1)}, u32[]{:S(2)}, u32[]{:S(2)}) collective-permute-start(f32[32,8,256]{2,1,0:T(8,128)S(1)} %all_to_all.16.refs_0_), channel_id=1, source_target_pairs={{0,2},{1,3},{2,4},{3,5},{4,6},{5,7},{6,0},{7,1},{8,10},{9,11},{10,... | collective-permute-start | bytes 786440 | tf_op jit(solution)/shard_map/ppermute | solution.py:245
  45.0 11.0 %collective-permute-start.1 = (f32[32,8,256]{2,1,0:T(8,128)S(1)}, f32[32,8,256]{2,1,0:T(8,128)S(1)}, u32[]{:S(2)}, u32[]{:S(2)}) collective-permute-start(f32[32,8,256]{2,1,0:T(8,128)S(1)} %all_to_all.16.refs_0_), channel_id=1, source_target_pairs={{0,4},{1,5},{2,6},{3,7},{4,0},{5,1},{6,2},{7,3},{8,12},{9,13},{10,... | collective-permute-start | bytes 786440 | tf_op jit(solution)/shard_map/ppermute | solution.py:245
  46.3 10.7 %collective-permute-start.4 = (f32[32,8,256]{2,1,0:T(8,128)S(1)}, f32[32,8,256]{2,1,0:T(8,128)S(1)}, u32[]{:S(2)}, u32[]{:S(2)}) collective-permute-start(f32[32,8,256]{2,1,0:T(8,128)S(1)} %all_to_all.16.refs_0_), channel_id=1, source_target_pairs={{0,1},{1,0},{2,3},{3,2},{4,5},{5,4},{6,7},{7,6},{8,9},{9,8},{10,11... | collective-permute-start | bytes 786440 | tf_op jit(solution)/shard_map/ppermute | solution.py:248
  50.7 6.5 %collective-permute-start.7 = (f32[32,8,256]{2,1,0:T(8,128)S(1)}, f32[32,8,256]{2,1,0:T(8,128)S(1)}, u32[]{:S(2)}, u32[]{:S(2)}) collective-permute-start(f32[32,8,256]{2,1,0:T(8,128)S(1)} %collective-permute-done.3.refs_3_), channel_id=1, source_target_pairs={{0,1},{1,0},{2,3},{3,2},{4,5},{5,4},{6,7},{7,6},{8,9},{9,8},{10,11... | collective-permute-start | bytes 786440 | tf_op jit(solution)/shard_map/ppermute | solution.py:248
  56.0 1.5 %collective-permute-start.6 = (f32[32,8,256]{2,1,0:T(8,128)S(1)}, f32[32,8,256]{2,1,0:T(8,128)S(1)}, u32[]{:S(2)}, u32[]{:S(2)}) collective-permute-start(f32[32,8,256]{2,1,0:T(8,128)S(1)} %collective-permute-done.2.refs_2_), channel_id=1, source_target_pairs={{0,1},{1,0},{2,3},{3,2},{4,5},{5,4},{6,7},{7,6},{8,9},{9,8},{10,11... | collective-permute-start | bytes 786440 | tf_op jit(solution)/shard_map/ppermute | solution.py:248
  56.0 1.9 %collective-permute-start.5 = (f32[32,8,256]{2,1,0:T(8,128)S(1)}, f32[32,8,256]{2,1,0:T(8,128)S(1)}, u32[]{:S(2)}, u32[]{:S(2)}) collective-permute-start(f32[32,8,256]{2,1,0:T(8,128)S(1)} %collective-permute-done.1.refs_1_), channel_id=1, source_target_pairs={{0,1},{1,0},{2,3},{3,2},{4,5},{5,4},{6,7},{7,6},{8,9},{9,8},{10,11... | collective-permute-start | bytes 786440 | tf_op jit(solution)/shard_map/ppermute | solution.py:248

commit v3 on v2

--- a/solution.py
+++ b/solution.py
@@ -12,6 +12,8 @@
 AHEAD = 10
 BLOCK = 64
 STEPS = (0, 2, 1, 3)
+SLOTS = 4
+ROOM = pltpu.CompilerParams(vmem_limit_bytes=24 << 20)
 
 
 def dot(a, b, dims, precision=None):
@@ -35,8 +37,7 @@
     return offset, counts_ref[index]
 
 
-def sketch_kernel(tensor_ref, counts_ref, scale_ref, samples_ref, keep_ref, send_ref, moved_ref,
-                  hadamard_ref, total_ref):
+def sketch_kernel(tensor_ref, counts_ref, scale_ref, samples_ref, total_ref, moved_ref, hadamard_ref):
     rows, slots, width = tensor_ref.shape
     total_slabs, sketch = samples_ref.shape
     index = lax.axis_index("yz")
@@ -59,10 +60,6 @@
         term = dot(scaled, hadamard_ref[slot], NN)
         total = total + jnp.where(slot < count, term, 0.0)
     total_ref[...] = total * (1.0 / (total_slabs * width) ** 0.5)
-    core = index % 2
-    half = rows // 2
-    keep_ref[...] = total_ref[pl.ds(pl.multiple_of(core * half, half), half), :]
-    send_ref[...] = total_ref[pl.ds(pl.multiple_of((1 - core) * half, half), half), :]
     chunk = 128 // slots
     for chunk_index in range(width // chunk):
         start = chunk_index * chunk
@@ -76,13 +73,12 @@
     sketch = samples.shape[1]
     chunks = width * slots // 128
     vmem = pl.BlockSpec(memory_space=pltpu.VMEM)
-    half = jax.ShapeDtypeStruct((rows // 2, sketch), F32)
     return pl.pallas_call(
         sketch_kernel,
-        out_shape=(half, half, jax.ShapeDtypeStruct((chunks, rows, 128), BF16)),
+        out_shape=(pltpu.VMEM((rows, sketch), F32), pltpu.VMEM((chunks, rows, 128), BF16)),
         in_specs=[vmem, pl.BlockSpec(memory_space=pltpu.SMEM), vmem, vmem],
-        out_specs=(vmem, vmem, vmem),
-        scratch_shapes=[pltpu.VMEM((slots, width, sketch), BF16), pltpu.VMEM((rows, sketch), F32)],
+        out_specs=(vmem, vmem),
+        scratch_shapes=[pltpu.VMEM((slots, width, sketch), BF16)],
         name="sketch",
     )(tensor, counts, scale, samples)
 
@@ -167,61 +163,102 @@
     return high, (array - high.astype(F32)).astype(BF16)
 
 
-def finish_kernel(*refs):
-    sources, (counts_ref, basis_ref, core_ref), scratch = refs[:9], refs[9:12], refs[12:]
-    work_ref, rows_ref, sems = scratch
-    blocks, parts, line, size = rows_ref.shape
-    chips = parts // 2
+def gram_of(pieces):
+    total = None
+    for piece in pieces:
+        flat = piece[...].reshape(-1, piece.shape[-1])
+        term = dot(flat, flat, TN, HIGHEST)
+        total = term if total is None else total + term
+    return total
+
+
+def gram_kernel(*refs):
+    refs[-1][...] = gram_of(refs[:-1])
+
+
+def factor_kernel(*refs):
+    pieces, gram_ref, (work_ref, rows_ref, sems) = refs[:8], refs[8], refs[9:]
+    members = len(pieces)
     index = lax.axis_index("yz")
     core, chip = index % 2, index // 2
-    places = [
-        which * chips + (chip + chips - step) % chips for which in (core, 1 - core) for step in STEPS
-    ]
-    copies = [
-        pltpu.make_async_copy(source, rows_ref.at[:, place], sems.at[number])
-        for number, (source, place) in enumerate(zip(sources[:8], places))
-    ]
-    for copy in copies:
-        copy.start()
-    gram = jnp.zeros((size, size), F32)
-    for source in sources[:8]:
-        piece = source[...].reshape(blocks * line, size)
-        gram = gram + dot(piece, piece, TN, HIGHEST)
-    work_ref[...] = gram
+    chips = members // 2
+    copies = []
+    for number, piece in enumerate(pieces):
+        which, step = divmod(number, chips)
+        place = 2 * ((chip + chips - STEPS[step]) % chips) + (core if which == 0 else 1 - core)
+        copies.append(pltpu.make_async_copy(piece, rows_ref.at[:, place], sems.at[number]))
+        copies[-1].start()
+    work_ref[...] = gram_ref[...] + gram_of(
+        [piece for number, piece in enumerate(pieces) if number % chips]
+    )
     invert_factor(work_ref)
     for copy in copies:
         copy.wait()
-    inverse = work_ref[...]
+
+
+def core_kernel(rows_ref, inverse_ref, moved_ref, counts_ref, basis_ref, core_ref):
+    blocks, parts, line, size = rows_ref.shape
+    inverse = inverse_ref[...]
     inverse_high, inverse_low = halves(inverse)
     block = rows_ref[lax.axis_index("gx")].reshape(parts * line, size)
     basis_ref[...] = dot(block, inverse, NT, HIGHEST)
     high, low = halves(rows_ref[...].reshape(blocks * parts * line, size))
     every = dot(high, inverse_high, NT) + dot(high, inverse_low, NT) + dot(low, inverse_high, NT)
-    result = dot(sources[8][...].reshape(blocks * parts * line, 128), every.astype(BF16), TN)
-    slots = 4
-    slot = lax.broadcasted_iota(I32, result.shape, 0) // (128 // slots)
-    core_ref[...] = jnp.where(slot < counts_ref[index], result, 0.0).astype(BF16)
-
-
-def finish(pieces, moved, counts):
-    blocks, rows, _ = moved.shape
-    line, size = pieces[0].shape[1:]
-    vmem = pl.BlockSpec(memory_space=pltpu.VMEM)
-    return pl.pallas_call(
-        finish_kernel,
+    result = dot(moved_ref[...].reshape(blocks * parts * line, 128), every.astype(BF16), TN)
+    slot = lax.broadcasted_iota(I32, result.shape, 0) // (128 // SLOTS)
+    live = slot < counts_ref[lax.axis_index("yz")]
+    core_ref[...] = jnp.where(live, result, 0.0).astype(BF16)
+
+
+def near(*arrays):
+    return tuple(pltpu.with_memory_space_constraint(each, pltpu.VMEM) for each in arrays)
+
+
+def gram_part(*pieces):
+    size = pieces[0].shape[-1]
+    vmem = pl.BlockSpec(memory_space=pltpu.VMEM)
+    return pl.pallas_call(
+        gram_kernel,
+        out_shape=pltpu.VMEM((size, size), F32),
+        in_specs=[vmem] * len(pieces),
+        out_specs=vmem,
+        name="gram",
+        compiler_params=ROOM,
+    )(*near(*pieces))
+
+
+def inverse_factor(pieces, gram):
+    blocks, line, size = pieces[0].shape
+    vmem = pl.BlockSpec(memory_space=pltpu.VMEM)
+    return pl.pallas_call(
+        factor_kernel,
         out_shape=(
-            jax.ShapeDtypeStruct((rows, size), F32),
+            jax.ShapeDtypeStruct((size, size), F32),
+            pltpu.VMEM((blocks, len(pieces), line, size), F32),
+        ),
+        in_specs=[vmem if number % len(STEPS) else pl.BlockSpec(memory_space=pl.ANY) for number in range(8)]
+        + [vmem],
+        out_specs=(vmem, vmem),
+        scratch_shapes=[pltpu.SemaphoreType.DMA((8,))],
+        name="factor",
+        compiler_params=ROOM,
+    )(*(near(piece)[0] if number % len(STEPS) else piece for number, piece in enumerate(pieces)), *near(gram))
+
+
+def core_and_basis(every, inverse, moved, counts):
+    _, parts, line, size = every.shape
+    vmem = pl.BlockSpec(memory_space=pltpu.VMEM)
+    return pl.pallas_call(
+        core_kernel,
+        out_shape=(
+            jax.ShapeDtypeStruct((parts * line, size), F32),
             jax.ShapeDtypeStruct((128, size), BF16),
         ),
-        in_specs=[vmem] * 9 + [pl.BlockSpec(memory_space=pltpu.SMEM)],
+        in_specs=[vmem, vmem, vmem, pl.BlockSpec(memory_space=pltpu.SMEM)],
         out_specs=(vmem, vmem),
-        scratch_shapes=[
-            pltpu.VMEM((size, size), F32),
-            pltpu.VMEM((blocks, rows // line, line, size), F32),
-            pltpu.SemaphoreType.DMA((8,)),
-        ],
-        name="finish",
-    )(*(pltpu.with_memory_space_constraint(each, pltpu.VMEM) for each in (*pieces, moved)), counts)
+        name="core",
+        compiler_params=ROOM,
+    )(*near(every), inverse, *near(moved), counts)
 
 
 def local(tensor_slabs, slab_counts, column_scale, samples):
@@ -229,14 +266,9 @@
     sketch = samples.shape[1]
     blocks = lax.axis_size("gx")
     members = lax.axis_size("yz")
-    chips = members // 2
     swap = [(j, j ^ 1) for j in range(members)]
-    same_core = [[2 * y + c for y in range(chips)] for c in range(2)]
-    keep, send, chunks = sketch_parts(tensor_slabs, slab_counts, column_scale, samples)
-    half = keep + lax.ppermute(send, "yz", swap)
-    parts = lax.all_to_all(
-        half.reshape(chips, -1, sketch), "yz", 0, 0, axis_index_groups=same_core, tiled=True
-    )
+    total, chunks = sketch_parts(tensor_slabs, slab_counts, column_scale, samples)
+    parts = lax.all_to_all(total.reshape(members, -1, sketch), "yz", 0, 0, tiled=True)
     part = jnp.broadcast_to(parts.sum(0), (blocks, *parts.shape[1:]))
     column = lax.all_to_all(part, "gx", 0, 0, tiled=True)
     pieces = [column]
@@ -246,7 +278,9 @@
     moved = lax.all_to_all(chunks, "gx", 0, 0, tiled=True)
     live = jnp.minimum(slab_counts, slots)
     pieces = pieces + [lax.ppermute(piece, "yz", swap) for piece in pieces]
-    basis, core = finish(pieces, moved, live)
+    gram = gram_part(pieces[0], pieces[len(STEPS)])
+    inverse, every = inverse_factor(pieces, gram)
+    basis, core = core_and_basis(every, inverse, moved, live)
     core = jnp.moveaxis(core.reshape(slots, -1, sketch), 2, 0)
     return basis, core
 

time: 74.7 us -> 72.2 us (0.967)
  waiting for transfers between devices: 11.9 us -> 10.2 us
  other arithmetic: 1.29 us -> 0.01 us
  blocking collectives: 31.2 us -> 32.4 us
  Pallas kernels: 18.1 us -> 17 us
    ppermute x1 -> x0, waiting for transfers between devices: 1.42 us -> none  [local(): half = keep + lax.ppermute(send, 'yz', swap)]
    pallas_call x2 -> x4, Pallas kernels: 18.1 us -> 17 us  [the longest x1 10.7 us: inverse_factor(): pl.pallas_call(factor_kernel, out_shape=(jax.ShapeDtypeStruct((size, size...]
    all_to_all x1, blocking collectives: 21.5 us -> 22.5 us  [local(): column = lax.all_to_all(part, 'gx', 0, 0, tiled=True)]
    ppermute x3, starting transfers between devices: 3.48 us -> 4.32 us  [local(): pieces.append(lax.ppermute(column, 'yz', turn))]
    reshape x1 -> x0, other arithmetic: 0.76 us -> none  [local(): half.reshape(chips, -1, sketch)]
  transfers between devices with their start and end apart: 9 -> 8, of which waited for: 6 -> 4; matrix products, arithmetic and copies ran while one was open for 1% -> 0% of each run, Pallas kernels for 0% -> 16%
where the time goes in v3:
time: 72.2 us; the launch traced here: 70.8 us
  blocking collectives  32.4 us (45%)
  Pallas kernels  17 us (24%)
  starting transfers between devices  10.4 us (14%)
  waiting for transfers between devices  10.2 us (14%)
    all_to_all x1, blocking collectives, local(): column = lax.all_to_all(part, 'gx', 0, 0, tiled=True)  22.5 us
    pallas_call x1, Pallas kernels, inverse_factor(): pl.pallas_call(factor_kernel, out_shape=(jax.ShapeDtypeStruct((size, size...  10.7 us
    all_to_all x1, blocking collectives, local(): lax.all_to_all(total.reshape(members, -1, sketch), 'yz', 0, 0, tiled=True)  9.88 us
    ppermute x3, waiting for transfers between devices, local(): pieces.append(lax.ppermute(column, 'yz', turn))  9.6 us
    all_to_all x1, starting transfers between devices, local(): moved = lax.all_to_all(chunks, 'gx', 0, 0, tiled=True)  5.57 us
    ppermute x3, starting transfers between devices, local(): pieces.append(lax.ppermute(column, 'yz', turn))  4.32 us
    pallas_call x1, Pallas kernels, sketch_parts(): pl.pallas_call(sketch_kernel, out_shape=(pltpu.VMEM((rows, sketch), F32),...  2.86 us
    pallas_call x1, Pallas kernels, core_and_basis(): pl.pallas_call(core_kernel, out_shape=(jax.ShapeDtypeStruct((parts * line...  2.7 us
  transfers between devices with their start and end apart: 8, of which 4 were waited for; matrix products, arithmetic and copies ran while one was open for 0% of the time, Pallas kernels for 16%

profile of v3, /device:TPU:2, one launch (start us, length us, event | category | flops | bytes accessed | tf_op | source)
XLA Modules:
  0.0 70.8 jit_solution(13242263175240766045)
XLA Ops:
  0.6 0.0 copy-start
  0.6 2.9 %sketch.1 = (f32[64,256]{1,0:T(8,128)S(1)}, bf16[32,64,128]{2,1,0:T(8,128)(2,1)}) custom-call(bf16[64,4,1024]{2,1,0:T(4,128)(2,1)} %tensor_ref.1, s32[8]{0:T(128)} %counts_ref.1, f32[16,1024]{1,0:T(8,128)} %scale_ref.1, s32[16,256]{1,0:T(8,128)} %samples_ref.1), custom_call_target="tpu_custom_call" | custom-call | tf_op jit(solution)/shard_map/sketch/pallas_call | solution.py:76
  3.5 9.9 %all_to_all.15 = f32[8,8,256]{2,1,0:T(8,128)S(1)} all-to-all(f32[8,8,256]{2,1,0:T(8,128)S(1)} %bitcast.4), channel_id=1, replica_groups=mesh['gx'=32,'yz'=8] {'yz'}, dimensions={0} | all-to-all | bytes 131072 | tf_op jit(solution)/shard_map/all_to_all | solution.py:271
  13.4 22.5 %all_to_all.16.refs_0_ = f32[32,8,256]{2,1,0:T(8,128)S(1)} all-to-all(f32[32,8,256]{2,1,0:T(8,128)S(1)} %broadcast_in_dim.3), channel_id=1, replica_groups=mesh['gx'=32,'yz'=8] {'gx'}, dimensions={0} | all-to-all | bytes 524288 | tf_op jit(solution)/shard_map/all_to_all | solution.py:273
  36.0 5.6 %all-to-all-start.2 = ((bf16[32,64,128]{2,1,0:T(8,128)(2,1)}), bf16[32,64,128]{2,1,0:T(8,128)(2,1)S(1)}, u32[]{:S(2)}, u32[]{:S(2)}) async-start(bf16[32,64,128]{2,1,0:T(8,128)(2,1)} %get-tuple-element.11), calls=%async_computation.2 | async-start | bytes 1048576 | tf_op jit(solution)/shard_map/all_to_all | solution.py:278
  41.5 1.1 %collective-permute-start = (f32[32,8,256]{2,1,0:T(8,128)S(1)}, f32[32,8,256]{2,1,0:T(8,128)S(1)}, u32[]{:S(2)}, u32[]{:S(2)}) collective-permute-start(f32[32,8,256]{2,1,0:T(8,128)S(1)} %all_to_all.16.refs_0_), channel_id=1, source_target_pairs={{0,4},{1,5},{2,6},{3,7},{4,0},{5,1},{6,2},{7,3},{8,12},{9,13},{10,... | collective-permute-start | bytes 786440 | tf_op jit(solution)/shard_map/ppermute | solution.py:277
  42.6 1.0 %collective-permute-start.1 = (f32[32,8,256]{2,1,0:T(8,128)S(1)}, f32[32,8,256]{2,1,0:T(8,128)S(1)}, u32[]{:S(2)}, u32[]{:S(2)}) collective-permute-start(f32[32,8,256]{2,1,0:T(8,128)S(1)} %all_to_all.16.refs_0_), channel_id=1, source_target_pairs={{0,2},{1,3},{2,4},{3,5},{4,6},{5,7},{6,0},{7,1},{8,10},{9,11},{10,... | collective-permute-start | bytes 786440 | tf_op jit(solution)/shard_map/ppermute | solution.py:277
  43.6 2.2 %collective-permute-start.2 = (f32[32,8,256]{2,1,0:T(8,128)S(1)}, f32[32,8,256]{2,1,0:T(8,128)S(1)}, u32[]{:S(2)}, u32[]{:S(2)}) collective-permute-start(f32[32,8,256]{2,1,0:T(8,128)S(1)} %all_to_all.16.refs_0_), channel_id=1, source_target_pairs={{0,6},{1,7},{2,0},{3,1},{4,2},{5,3},{6,4},{7,5},{8,14},{9,15},{10,... | collective-permute-start | bytes 786440 | tf_op jit(solution)/shard_map/ppermute | solution.py:277
  45.8 0.0 collective-permute-start.3
  45.8 6.4 %collective-permute-done.refs_1_ = f32[32,8,256]{2,1,0:T(8,128)S(1)} collective-permute-done((f32[32,8,256]{2,1,0:T(8,128)S(1)}, f32[32,8,256]{2,1,0:T(8,128)S(1)}, u32[]{:S(2)}, u32[]{:S(2)}) %collective-permute-start) | collective-permute-done | bytes 262176 | tf_op jit(solution)/shard_map/ppermute | solution.py:277
  52.3 0.0 collective-permute-start.4
  52.3 3.2 %collective-permute-done.1.refs_2_ = f32[32,8,256]{2,1,0:T(8,128)S(1)} collective-permute-done((f32[32,8,256]{2,1,0:T(8,128)S(1)}, f32[32,8,256]{2,1,0:T(8,128)S(1)}, u32[]{:S(2)}, u32[]{:S(2)}) %collective-permute-start.1) | collective-permute-done | bytes 262176 | tf_op jit(solution)/shard_map/ppermute | solution.py:277
  55.5 0.0 collective-permute-start.5
  55.5 0.0 collective-permute-done.2.refs_3_
  55.5 0.5 collective-permute-start.6
  56.0 0.0 copy-done
  56.0 0.0 collective-permute-done.3.refs_1_.refs_4_
  56.0 0.7 %gram.1.refs_8_ = f32[256,256]{1,0:T(8,128)S(1)} custom-call(f32[32,8,256]{2,1,0:T(8,128)S(1)} %all_to_all.16.refs_0_, f32[32,8,256]{2,1,0:T(8,128)S(1)} %collective-permute-done.3.refs_1_.refs_4_), custom_call_target="tpu_custom_call" | custom-call | tf_op jit(solution)/shard_map/gram/pallas_call | solution.py:220
  56.7 0.0 collective-permute-done.4.refs_5_
  56.7 0.3 collective-permute-done.5.refs_6_
  57.0 0.4 collective-permute-done.6.refs_7_
  57.4 10.7 %factor.1 = (f32[256,256]{1,0:T(8,128)S(1)}, f32[32,8,8,256]{3,2,1,0:T(8,128)S(1)}) custom-call(f32[32,8,256]{2,1,0:T(8,128)S(1)} %all_to_all.16.refs_0_, f32[32,8,256]{2,1,0:T(8,128)S(1)} %collective-permute-done.refs_1_, f32[32,8,256]{2,1,0:T(8,128)S(1)} %collective-permute-done.1.refs_2_, f32[32,8,256]{2,1,0:T(8,128)S(1)} %collective-permute-done.2.refs_3_, ...), custom_call_target="tpu_custom_call" | custom-call | tf_op jit(solution)/shard_map/factor/pallas_call | solution.py:233
  68.1 0.0 all-to-all-done.2.moved_ref
  68.1 2.7 %core.1 = (f32[64,256]{1,0:T(8,128)}, bf16[128,256]{1,0:T(8,128)(2,1)}) custom-call(f32[32,8,8,256]{3,2,1,0:T(8,128)S(1)} %get-tuple-element.9.rows_ref, f32[256,256]{1,0:T(8,128)S(1)} %get-tuple-element.10.inverse_ref, bf16[32,64,128]{2,1,0:T(8,128)(2,1)S(1)} %all-to-all-done.2.moved_ref, s32[8]{0:T(128)S(1)} %broadcast_minimum_fusion.counts_ref), custom_call_target="tpu_custom_call" | custom-call | tf_op jit(solution)/shard_map/core/pallas_call | solution.py:251
  (3 shorter events, 0.0 us)
Async XLA Ops:
  0.6 55.3 %copy-start = (s32[8]{0:T(128)S(1)}, s32[8]{0:T(128)}, u32[]{:S(2)}) copy-start(s32[8]{0:T(128)} %counts_ref.1) | copy-start | bytes 100
  36.0 32.1 %all-to-all-start.2 = ((bf16[32,64,128]{2,1,0:T(8,128)(2,1)}), bf16[32,64,128]{2,1,0:T(8,128)(2,1)S(1)}, u32[]{:S(2)}, u32[]{:S(2)}) async-start(bf16[32,64,128]{2,1,0:T(8,128)(2,1)} %get-tuple-element.11), calls=%async_computation.2 | async-start | bytes 1048576 | tf_op jit(solution)/shard_map/all_to_all | solution.py:278
  41.5 10.8 %collective-permute-start = (f32[32,8,256]{2,1,0:T(8,128)S(1)}, f32[32,8,256]{2,1,0:T(8,128)S(1)}, u32[]{:S(2)}, u32[]{:S(2)}) collective-permute-start(f32[32,8,256]{2,1,0:T(8,128)S(1)} %all_to_all.16.refs_0_), channel_id=1, source_target_pairs={{0,4},{1,5},{2,6},{3,7},{4,0},{5,1},{6,2},{7,3},{8,12},{9,13},{10,... | collective-permute-start | bytes 786440 | tf_op jit(solution)/shard_map/ppermute | solution.py:277
  42.6 12.8 %collective-permute-start.1 = (f32[32,8,256]{2,1,0:T(8,128)S(1)}, f32[32,8,256]{2,1,0:T(8,128)S(1)}, u32[]{:S(2)}, u32[]{:S(2)}) collective-permute-start(f32[32,8,256]{2,1,0:T(8,128)S(1)} %all_to_all.16.refs_0_), channel_id=1, source_target_pairs={{0,2},{1,3},{2,4},{3,5},{4,6},{5,7},{6,0},{7,1},{8,10},{9,11},{10,... | collective-permute-start | bytes 786440 | tf_op jit(solution)/shard_map/ppermute | solution.py:277
  43.6 11.8 %collective-permute-start.2 = (f32[32,8,256]{2,1,0:T(8,128)S(1)}, f32[32,8,256]{2,1,0:T(8,128)S(1)}, u32[]{:S(2)}, u32[]{:S(2)}) collective-permute-start(f32[32,8,256]{2,1,0:T(8,128)S(1)} %all_to_all.16.refs_0_), channel_id=1, source_target_pairs={{0,6},{1,7},{2,0},{3,1},{4,2},{5,3},{6,4},{7,5},{8,14},{9,15},{10,... | collective-permute-start | bytes 786440 | tf_op jit(solution)/shard_map/ppermute | solution.py:277
  45.8 10.1 %collective-permute-start.3 = (f32[32,8,256]{2,1,0:T(8,128)S(1)}, f32[32,8,256]{2,1,0:T(8,128)S(1)}, u32[]{:S(2)}, u32[]{:S(2)}) collective-permute-start(f32[32,8,256]{2,1,0:T(8,128)S(1)} %all_to_all.16.refs_0_), channel_id=1, source_target_pairs={{0,1},{1,0},{2,3},{3,2},{4,5},{5,4},{6,7},{7,6},{8,9},{9,8},{10,11... | collective-permute-start | bytes 786440 | tf_op jit(solution)/shard_map/ppermute | solution.py:280
  52.3 4.4 %collective-permute-start.4 = (f32[32,8,256]{2,1,0:T(8,128)S(1)}, f32[32,8,256]{2,1,0:T(8,128)S(1)}, u32[]{:S(2)}, u32[]{:S(2)}) collective-permute-start(f32[32,8,256]{2,1,0:T(8,128)S(1)} %collective-permute-done.refs_1_), channel_id=1, source_target_pairs={{0,1},{1,0},{2,3},{3,2},{4,5},{5,4},{6,7},{7,6},{8,9},{9,8},{10,11... | collective-permute-start | bytes 786440 | tf_op jit(solution)/shard_map/ppermute | solution.py:280
  55.5 1.5 %collective-permute-start.5 = (f32[32,8,256]{2,1,0:T(8,128)S(1)}, f32[32,8,256]{2,1,0:T(8,128)S(1)}, u32[]{:S(2)}, u32[]{:S(2)}) collective-permute-start(f32[32,8,256]{2,1,0:T(8,128)S(1)} %collective-permute-done.1.refs_2_), channel_id=1, source_target_pairs={{0,1},{1,0},{2,3},{3,2},{4,5},{5,4},{6,7},{7,6},{8,9},{9,8},{10,11... | collective-permute-start | bytes 786440 | tf_op jit(solution)/shard_map/ppermute | solution.py:280
  55.5 1.9 %collective-permute-start.6 = (f32[32,8,256]{2,1,0:T(8,128)S(1)}, f32[32,8,256]{2,1,0:T(8,128)S(1)}, u32[]{:S(2)}, u32[]{:S(2)}) collective-permute-start(f32[32,8,256]{2,1,0:T(8,128)S(1)} %collective-permute-done.2.refs_3_), channel_id=1, source_target_pairs={{0,1},{1,0},{2,3},{3,2},{4,5},{5,4},{6,7},{7,6},{8,9},{9,8},{10,11... | collective-permute-start | bytes 786440 | tf_op jit(solution)/shard_map/ppermute | solution.py:280

commit v4 on v3

--- a/solution.py
+++ b/solution.py
@@ -13,6 +13,7 @@
 BLOCK = 64
 STEPS = (0, 2, 1, 3)
 SLOTS = 4
+SHARES = 4
 ROOM = pltpu.CompilerParams(vmem_limit_bytes=24 << 20)
 
 
@@ -75,7 +76,7 @@
     vmem = pl.BlockSpec(memory_space=pltpu.VMEM)
     return pl.pallas_call(
         sketch_kernel,
-        out_shape=(pltpu.VMEM((rows, sketch), F32), pltpu.VMEM((chunks, rows, 128), BF16)),
+        out_shape=(pltpu.VMEM((rows, sketch), F32), jax.ShapeDtypeStruct((chunks, rows, 128), BF16)),
         in_specs=[vmem, pl.BlockSpec(memory_space=pltpu.SMEM), vmem, vmem],
         out_specs=(vmem, vmem),
         scratch_shapes=[pltpu.VMEM((slots, width, sketch), BF16)],
@@ -164,12 +165,16 @@
 
 
 def gram_of(pieces):
-    total = None
+    square = cross = None
     for piece in pieces:
         flat = piece[...].reshape(-1, piece.shape[-1])
-        term = dot(flat, flat, TN, HIGHEST)
-        total = term if total is None else total + term
-    return total
+        high, rest = halves(flat)
+        low = (flat - high.astype(F32) - rest.astype(F32)).astype(BF16)
+        even = dot(high, high, TN) + dot(rest, rest, TN)
+        odd = dot(high, rest, TN) + dot(high, low, TN)
+        square = even if square is None else square + even
+        cross = odd if cross is None else cross + odd
+    return square + (cross + cross.T)
 
 
 def gram_kernel(*refs):
@@ -196,15 +201,33 @@
         copy.wait()
 
 
-def core_kernel(rows_ref, inverse_ref, moved_ref, counts_ref, basis_ref, core_ref):
+def core_kernel(rows_any, inverse_ref, moved_any, counts_ref, basis_ref, core_ref,
+                rows_ref, moved_ref, block_ref, sems):
     blocks, parts, line, size = rows_ref.shape
+    share = blocks // SHARES
+    own = pltpu.make_async_copy(rows_any.at[lax.axis_index("gx")], block_ref, sems.at[SHARES + 1])
+    whole = pltpu.make_async_copy(moved_any, moved_ref, sems.at[SHARES])
+    copies = []
+    for number in range(SHARES):
+        place = pl.ds(number * share, share)
+        copies.append(
+            pltpu.make_async_copy(rows_any.at[place], rows_ref.at[place], sems.at[number])
+        )
+    for copy in (own, *copies, whole):
+        copy.start()
     inverse = inverse_ref[...]
     inverse_high, inverse_low = halves(inverse)
-    block = rows_ref[lax.axis_index("gx")].reshape(parts * line, size)
-    basis_ref[...] = dot(block, inverse, NT, HIGHEST)
-    high, low = halves(rows_ref[...].reshape(blocks * parts * line, size))
-    every = dot(high, inverse_high, NT) + dot(high, inverse_low, NT) + dot(low, inverse_high, NT)
-    result = dot(moved_ref[...].reshape(blocks * parts * line, 128), every.astype(BF16), TN)
+    own.wait()
+    basis_ref[...] = dot(block_ref[...].reshape(parts * line, size), inverse, NT, HIGHEST)
+    result = jnp.zeros((128, size), F32)
+    for number, copy in enumerate(copies):
+        copy.wait()
+        place = slice(number * share, (number + 1) * share)
+        high, low = halves(rows_ref[place].reshape(share * parts * line, size))
+        every = dot(high, inverse_high, NT) + dot(high, inverse_low, NT) + dot(low, inverse_high, NT)
+        if number == 0:
+            whole.wait()
+        result = result + dot(moved_ref[place].reshape(share * parts * line, 128), every.astype(BF16), TN)
     slot = lax.broadcasted_iota(I32, result.shape, 0) // (128 // SLOTS)
     live = slot < counts_ref[lax.axis_index("yz")]
     core_ref[...] = jnp.where(live, result, 0.0).astype(BF16)
@@ -233,12 +256,12 @@
     return pl.pallas_call(
         factor_kernel,
         out_shape=(
-            jax.ShapeDtypeStruct((size, size), F32),
-            pltpu.VMEM((blocks, len(pieces), line, size), F32),
+            pltpu.HBM((size, size), F32),
+            pltpu.HBM((blocks, len(pieces), line, size), F32),
         ),
         in_specs=[vmem if number % len(STEPS) else pl.BlockSpec(memory_space=pl.ANY) for number in range(8)]
         + [vmem],
-        out_specs=(vmem, vmem),
+        out_specs=(vmem, pl.BlockSpec(memory_space=pl.ANY)),
         scratch_shapes=[pltpu.SemaphoreType.DMA((8,))],
         name="factor",
         compiler_params=ROOM,
@@ -248,17 +271,24 @@
 def core_and_basis(every, inverse, moved, counts):
     _, parts, line, size = every.shape
     vmem = pl.BlockSpec(memory_space=pltpu.VMEM)
+    free = pl.BlockSpec(memory_space=pl.ANY)
     return pl.pallas_call(
         core_kernel,
         out_shape=(
             jax.ShapeDtypeStruct((parts * line, size), F32),
             jax.ShapeDtypeStruct((128, size), BF16),
         ),
-        in_specs=[vmem, vmem, vmem, pl.BlockSpec(memory_space=pltpu.SMEM)],
+        in_specs=[free, vmem, free, pl.BlockSpec(memory_space=pltpu.SMEM)],
         out_specs=(vmem, vmem),
+        scratch_shapes=[
+            pltpu.VMEM(every.shape, F32),
+            pltpu.VMEM(moved.shape, BF16),
+            pltpu.VMEM((parts, line, size), F32),
+            pltpu.SemaphoreType.DMA((SHARES + 2,)),
+        ],
         name="core",
         compiler_params=ROOM,
-    )(*near(every), inverse, *near(moved), counts)
+    )(*(pltpu.with_memory_space_constraint(each, pltpu.HBM) for each in (every, inverse)), moved, counts)
 
 
 def local(tensor_slabs, slab_counts, column_scale, samples):

time: 72.2 us -> 75.7 us (1.048)
  Pallas kernels: 17 us -> 20.1 us
    pallas_call x1, Pallas kernels: 2.7 us -> 5.65 us  [core_and_basis(): pl.pallas_call(core_kernel, out_shape=(jax.ShapeDtypeStruct((parts * line...]
where the time goes in v4:
time: 75.7 us; the launch traced here: 74.2 us
  blocking collectives  32.4 us (43%)
  Pallas kernels  20.1 us (27%)
  starting transfers between devices  10.4 us (14%)
  waiting for transfers between devices  10.4 us (14%)
  between operations  0.86 us (1%)
    all_to_all x1, blocking collectives, local(): column = lax.all_to_all(part, 'gx', 0, 0, tiled=True)  22.5 us
    pallas_call x1, Pallas kernels, inverse_factor(): pl.pallas_call(factor_kernel, out_shape=(pltpu.HBM((size, size), F32), pl...  11 us
    all_to_all x1, blocking collectives, local(): lax.all_to_all(total.reshape(members, -1, sketch), 'yz', 0, 0, tiled=True)  9.88 us
    ppermute x3, waiting for transfers between devices, local(): pieces.append(lax.ppermute(column, 'yz', turn))  9.6 us
    pallas_call x1, Pallas kernels, core_and_basis(): pl.pallas_call(core_kernel, out_shape=(jax.ShapeDtypeStruct((parts * line...  5.65 us
    all_to_all x1, starting transfers between devices, local(): moved = lax.all_to_all(chunks, 'gx', 0, 0, tiled=True)  5.57 us
    ppermute x3, starting transfers between devices, local(): pieces.append(lax.ppermute(column, 'yz', turn))  4.32 us
    pallas_call x1, Pallas kernels, sketch_parts(): pl.pallas_call(sketch_kernel, out_shape=(pltpu.VMEM((rows, sketch), F32),...  2.88 us
  transfers between devices with their start and end apart: 8, of which 4 were waited for; matrix products, arithmetic and copies ran while one was open for 0% of the time, Pallas kernels for 16%

profile of v4, /device:TPU:2, one launch (start us, length us, event | category | flops | bytes accessed | tf_op | source)
XLA Modules:
  0.0 74.2 jit_solution(14515853551767429613)
XLA Ops:
  0.6 0.0 copy-start
  0.6 2.9 %sketch.1 = (f32[64,256]{1,0:T(8,128)S(1)}, bf16[32,64,128]{2,1,0:T(8,128)(2,1)}) custom-call(bf16[64,4,1024]{2,1,0:T(4,128)(2,1)} %tensor_ref.1, s32[8]{0:T(128)} %counts_ref.1, f32[16,1024]{1,0:T(8,128)} %scale_ref.1, s32[16,256]{1,0:T(8,128)} %samples_ref.1), custom_call_target="tpu_custom_call" | custom-call | tf_op jit(solution)/shard_map/sketch/pallas_call | solution.py:77
  3.5 9.9 %all_to_all.15 = f32[8,8,256]{2,1,0:T(8,128)S(1)} all-to-all(f32[8,8,256]{2,1,0:T(8,128)S(1)} %bitcast.4), channel_id=1, replica_groups=mesh['gx'=32,'yz'=8] {'yz'}, dimensions={0} | all-to-all | bytes 131072 | tf_op jit(solution)/shard_map/all_to_all | solution.py:301
  13.4 22.5 %all_to_all.16.refs_0_ = f32[32,8,256]{2,1,0:T(8,128)S(1)} all-to-all(f32[32,8,256]{2,1,0:T(8,128)S(1)} %broadcast_in_dim.3), channel_id=1, replica_groups=mesh['gx'=32,'yz'=8] {'gx'}, dimensions={0} | all-to-all | bytes 524288 | tf_op jit(solution)/shard_map/all_to_all | solution.py:303
  36.0 5.6 %all-to-all-start.2 = ((bf16[32,64,128]{2,1,0:T(8,128)(2,1)}), bf16[32,64,128]{2,1,0:T(8,128)(2,1)S(1)}, u32[]{:S(2)}, u32[]{:S(2)}) async-start(bf16[32,64,128]{2,1,0:T(8,128)(2,1)} %get-tuple-element.11), calls=%async_computation.2 | async-start | bytes 1048576 | tf_op jit(solution)/shard_map/all_to_all | solution.py:308
  41.5 1.1 %collective-permute-start = (f32[32,8,256]{2,1,0:T(8,128)S(1)}, f32[32,8,256]{2,1,0:T(8,128)S(1)}, u32[]{:S(2)}, u32[]{:S(2)}) collective-permute-start(f32[32,8,256]{2,1,0:T(8,128)S(1)} %all_to_all.16.refs_0_), channel_id=1, source_target_pairs={{0,4},{1,5},{2,6},{3,7},{4,0},{5,1},{6,2},{7,3},{8,12},{9,13},{10,... | collective-permute-start | bytes 786440 | tf_op jit(solution)/shard_map/ppermute | solution.py:307
  42.6 1.0 %collective-permute-start.1 = (f32[32,8,256]{2,1,0:T(8,128)S(1)}, f32[32,8,256]{2,1,0:T(8,128)S(1)}, u32[]{:S(2)}, u32[]{:S(2)}) collective-permute-start(f32[32,8,256]{2,1,0:T(8,128)S(1)} %all_to_all.16.refs_0_), channel_id=1, source_target_pairs={{0,2},{1,3},{2,4},{3,5},{4,6},{5,7},{6,0},{7,1},{8,10},{9,11},{10,... | collective-permute-start | bytes 786440 | tf_op jit(solution)/shard_map/ppermute | solution.py:307
  43.7 2.2 %collective-permute-start.2 = (f32[32,8,256]{2,1,0:T(8,128)S(1)}, f32[32,8,256]{2,1,0:T(8,128)S(1)}, u32[]{:S(2)}, u32[]{:S(2)}) collective-permute-start(f32[32,8,256]{2,1,0:T(8,128)S(1)} %all_to_all.16.refs_0_), channel_id=1, source_target_pairs={{0,6},{1,7},{2,0},{3,1},{4,2},{5,3},{6,4},{7,5},{8,14},{9,15},{10,... | collective-permute-start | bytes 786440 | tf_op jit(solution)/shard_map/ppermute | solution.py:307
  45.9 0.0 collective-permute-start.3
  45.9 6.4 %collective-permute-done.refs_1_ = f32[32,8,256]{2,1,0:T(8,128)S(1)} collective-permute-done((f32[32,8,256]{2,1,0:T(8,128)S(1)}, f32[32,8,256]{2,1,0:T(8,128)S(1)}, u32[]{:S(2)}, u32[]{:S(2)}) %collective-permute-start) | collective-permute-done | bytes 262176 | tf_op jit(solution)/shard_map/ppermute | solution.py:307
  52.3 0.0 collective-permute-start.4
  52.3 3.2 %collective-permute-done.1.refs_2_ = f32[32,8,256]{2,1,0:T(8,128)S(1)} collective-permute-done((f32[32,8,256]{2,1,0:T(8,128)S(1)}, f32[32,8,256]{2,1,0:T(8,128)S(1)}, u32[]{:S(2)}, u32[]{:S(2)}) %collective-permute-start.1) | collective-permute-done | bytes 262176 | tf_op jit(solution)/shard_map/ppermute | solution.py:307
  55.5 0.0 collective-permute-start.5
  55.5 0.0 collective-permute-done.2.refs_3_
  55.5 0.5 collective-permute-start.6
  56.0 0.0 copy-done
  56.0 0.0 collective-permute-done.3.refs_1_.refs_4_
  56.0 0.5 gram.1.refs_8_
  56.5 0.0 collective-permute-done.4.refs_5_
  56.5 0.5 collective-permute-done.5.refs_6_
  57.0 0.4 collective-permute-done.6.refs_7_
  57.4 11.0 %factor.1 = (f32[256,256]{1,0:T(8,128)}, f32[32,8,8,256]{3,2,1,0:T(8,128)}) custom-call(f32[32,8,256]{2,1,0:T(8,128)S(1)} %all_to_all.16.refs_0_, f32[32,8,256]{2,1,0:T(8,128)S(1)} %collective-permute-done.refs_1_, f32[32,8,256]{2,1,0:T(8,128)S(1)} %collective-permute-done.1.refs_2_, f32[32,8,256]{2,1,0:T(8,128)S(1)} %collective-permute-done.2.refs_3_, ...), custom_call_target="tpu_custom_call" | custom-call | tf_op jit(solution)/shard_map/factor/pallas_call | solution.py:256
  68.4 0.0 all-to-all-done.2.moved_any
  68.4 5.6 %core.1 = (f32[64,256]{1,0:T(8,128)}, bf16[128,256]{1,0:T(8,128)(2,1)}) custom-call(f32[32,8,8,256]{3,2,1,0:T(8,128)} %get-tuple-element.9.rows_any, f32[256,256]{1,0:T(8,128)} %get-tuple-element.10.inverse_ref, bf16[32,64,128]{2,1,0:T(8,128)(2,1)S(1)} %all-to-all-done.2.moved_any, s32[8]{0:T(128)S(1)} %broadcast_minimum_fusion.counts_ref), custom_call_target="tpu_custom_call" | custom-call | tf_op jit(solution)/shard_map/core/pallas_call | solution.py:275
  (3 shorter events, 0.0 us)
Async XLA Ops:
  0.6 55.4 %copy-start = (s32[8]{0:T(128)S(1)}, s32[8]{0:T(128)}, u32[]{:S(2)}) copy-start(s32[8]{0:T(128)} %counts_ref.1) | copy-start | bytes 100
  36.0 32.5 %all-to-all-start.2 = ((bf16[32,64,128]{2,1,0:T(8,128)(2,1)}), bf16[32,64,128]{2,1,0:T(8,128)(2,1)S(1)}, u32[]{:S(2)}, u32[]{:S(2)}) async-start(bf16[32,64,128]{2,1,0:T(8,128)(2,1)} %get-tuple-element.11), calls=%async_computation.2 | async-start | bytes 1048576 | tf_op jit(solution)/shard_map/all_to_all | solution.py:308
  41.5 10.8 %collective-permute-start = (f32[32,8,256]{2,1,0:T(8,128)S(1)}, f32[32,8,256]{2,1,0:T(8,128)S(1)}, u32[]{:S(2)}, u32[]{:S(2)}) collective-permute-start(f32[32,8,256]{2,1,0:T(8,128)S(1)} %all_to_all.16.refs_0_), channel_id=1, source_target_pairs={{0,4},{1,5},{2,6},{3,7},{4,0},{5,1},{6,2},{7,3},{8,12},{9,13},{10,... | collective-permute-start | bytes 786440 | tf_op jit(solution)/shard_map/ppermute | solution.py:307
  42.6 12.8 %collective-permute-start.1 = (f32[32,8,256]{2,1,0:T(8,128)S(1)}, f32[32,8,256]{2,1,0:T(8,128)S(1)}, u32[]{:S(2)}, u32[]{:S(2)}) collective-permute-start(f32[32,8,256]{2,1,0:T(8,128)S(1)} %all_to_all.16.refs_0_), channel_id=1, source_target_pairs={{0,2},{1,3},{2,4},{3,5},{4,6},{5,7},{6,0},{7,1},{8,10},{9,11},{10,... | collective-permute-start | bytes 786440 | tf_op jit(solution)/shard_map/ppermute | solution.py:307
  43.7 11.8 %collective-permute-start.2 = (f32[32,8,256]{2,1,0:T(8,128)S(1)}, f32[32,8,256]{2,1,0:T(8,128)S(1)}, u32[]{:S(2)}, u32[]{:S(2)}) collective-permute-start(f32[32,8,256]{2,1,0:T(8,128)S(1)} %all_to_all.16.refs_0_), channel_id=1, source_target_pairs={{0,6},{1,7},{2,0},{3,1},{4,2},{5,3},{6,4},{7,5},{8,14},{9,15},{10,... | collective-permute-start | bytes 786440 | tf_op jit(solution)/shard_map/ppermute | solution.py:307
  45.9 10.1 %collective-permute-start.3 = (f32[32,8,256]{2,1,0:T(8,128)S(1)}, f32[32,8,256]{2,1,0:T(8,128)S(1)}, u32[]{:S(2)}, u32[]{:S(2)}) collective-permute-start(f32[32,8,256]{2,1,0:T(8,128)S(1)} %all_to_all.16.refs_0_), channel_id=1, source_target_pairs={{0,1},{1,0},{2,3},{3,2},{4,5},{5,4},{6,7},{7,6},{8,9},{9,8},{10,11... | collective-permute-start | bytes 786440 | tf_op jit(solution)/shard_map/ppermute | solution.py:310
  52.3 4.2 %collective-permute-start.4 = (f32[32,8,256]{2,1,0:T(8,128)S(1)}, f32[32,8,256]{2,1,0:T(8,128)S(1)}, u32[]{:S(2)}, u32[]{:S(2)}) collective-permute-start(f32[32,8,256]{2,1,0:T(8,128)S(1)} %collective-permute-done.refs_1_), channel_id=1, source_target_pairs={{0,1},{1,0},{2,3},{3,2},{4,5},{5,4},{6,7},{7,6},{8,9},{9,8},{10,11... | collective-permute-start | bytes 786440 | tf_op jit(solution)/shard_map/ppermute | solution.py:310
  55.5 1.5 %collective-permute-start.5 = (f32[32,8,256]{2,1,0:T(8,128)S(1)}, f32[32,8,256]{2,1,0:T(8,128)S(1)}, u32[]{:S(2)}, u32[]{:S(2)}) collective-permute-start(f32[32,8,256]{2,1,0:T(8,128)S(1)} %collective-permute-done.1.refs_2_), channel_id=1, source_target_pairs={{0,1},{1,0},{2,3},{3,2},{4,5},{5,4},{6,7},{7,6},{8,9},{9,8},{10,11... | collective-permute-start | bytes 786440 | tf_op jit(solution)/shard_map/ppermute | solution.py:310
  55.5 1.9 %collective-permute-start.6 = (f32[32,8,256]{2,1,0:T(8,128)S(1)}, f32[32,8,256]{2,1,0:T(8,128)S(1)}, u32[]{:S(2)}, u32[]{:S(2)}) collective-permute-start(f32[32,8,256]{2,1,0:T(8,128)S(1)} %collective-permute-done.2.refs_3_), channel_id=1, source_target_pairs={{0,1},{1,0},{2,3},{3,2},{4,5},{5,4},{6,7},{7,6},{8,9},{9,8},{10,11... | collective-permute-start | bytes 786440 | tf_op jit(solution)/shard_map/ppermute | solution.py:310

commit v5 on v3

--- a/solution.py
+++ b/solution.py
@@ -75,7 +75,7 @@
     vmem = pl.BlockSpec(memory_space=pltpu.VMEM)
     return pl.pallas_call(
         sketch_kernel,
-        out_shape=(pltpu.VMEM((rows, sketch), F32), pltpu.VMEM((chunks, rows, 128), BF16)),
+        out_shape=(pltpu.VMEM((rows, sketch), F32), jax.ShapeDtypeStruct((chunks, rows, 128), BF16)),
         in_specs=[vmem, pl.BlockSpec(memory_space=pltpu.SMEM), vmem, vmem],
         out_specs=(vmem, vmem),
         scratch_shapes=[pltpu.VMEM((slots, width, sketch), BF16)],
@@ -164,12 +164,16 @@
 
 
 def gram_of(pieces):
-    total = None
+    square = cross = None
     for piece in pieces:
         flat = piece[...].reshape(-1, piece.shape[-1])
-        term = dot(flat, flat, TN, HIGHEST)
-        total = term if total is None else total + term
-    return total
+        high, rest = halves(flat)
+        low = (flat - high.astype(F32) - rest.astype(F32)).astype(BF16)
+        even = dot(high, high, TN) + dot(rest, rest, TN)
+        odd = dot(high, rest, TN) + dot(high, low, TN)
+        square = even if square is None else square + even
+        cross = odd if cross is None else cross + odd
+    return square + (cross + cross.T)
 
 
 def gram_kernel(*refs):
@@ -177,37 +181,32 @@
 
 
 def factor_kernel(*refs):
-    pieces, gram_ref, (work_ref, rows_ref, sems) = refs[:8], refs[8], refs[9:]
-    members = len(pieces)
+    pieces, gram_ref, inverse_ref = refs[:-2], refs[-2], refs[-1]
+    inverse_ref[...] = gram_ref[...] + gram_of(pieces)
+    invert_factor(inverse_ref)
+
+
+def core_kernel(*refs):
+    pieces, (inverse_ref, moved_ref, counts_ref, basis_ref, core_ref), scratch = refs[:8], refs[8:13], refs[13:]
+    rows_ref, block_ref = scratch
+    blocks, parts, line, size = rows_ref.shape
     index = lax.axis_index("yz")
     core, chip = index % 2, index // 2
-    chips = members // 2
-    copies = []
+    chips = parts // 2
+    inverse = inverse_ref[...]
+    inverse_high, inverse_low = halves(inverse)
     for number, piece in enumerate(pieces):
         which, step = divmod(number, chips)
         place = 2 * ((chip + chips - STEPS[step]) % chips) + (core if which == 0 else 1 - core)
-        copies.append(pltpu.make_async_copy(piece, rows_ref.at[:, place], sems.at[number]))
-        copies[-1].start()
-    work_ref[...] = gram_ref[...] + gram_of(
-        [piece for number, piece in enumerate(pieces) if number % chips]
-    )
-    invert_factor(work_ref)
-    for copy in copies:
-        copy.wait()
-
-
-def core_kernel(rows_ref, inverse_ref, moved_ref, counts_ref, basis_ref, core_ref):
-    blocks, parts, line, size = rows_ref.shape
-    inverse = inverse_ref[...]
-    inverse_high, inverse_low = halves(inverse)
-    block = rows_ref[lax.axis_index("gx")].reshape(parts * line, size)
-    basis_ref[...] = dot(block, inverse, NT, HIGHEST)
-    high, low = halves(rows_ref[...].reshape(blocks * parts * line, size))
-    every = dot(high, inverse_high, NT) + dot(high, inverse_low, NT) + dot(low, inverse_high, NT)
-    result = dot(moved_ref[...].reshape(blocks * parts * line, 128), every.astype(BF16), TN)
+        block_ref[place] = piece[lax.axis_index("gx")]
+        high, low = halves(piece[...].reshape(blocks * line, size))
+        rows = dot(high, inverse_high, NT) + dot(high, inverse_low, NT) + dot(low, inverse_high, NT)
+        rows_ref[:, place] = rows.reshape(blocks, line, size)
+    basis_ref[...] = dot(block_ref[...].reshape(parts * line, size), inverse, NT, HIGHEST)
+    every = rows_ref[...].reshape(blocks * parts * line, size).astype(BF16)
+    result = dot(moved_ref[...].reshape(blocks * parts * line, 128), every, TN)
     slot = lax.broadcasted_iota(I32, result.shape, 0) // (128 // SLOTS)
-    live = slot < counts_ref[lax.axis_index("yz")]
-    core_ref[...] = jnp.where(live, result, 0.0).astype(BF16)
+    core_ref[...] = jnp.where(slot < counts_ref[index], result, 0.0).astype(BF16)
 
 
 def near(*arrays):
@@ -228,25 +227,21 @@
 
 
 def inverse_factor(pieces, gram):
-    blocks, line, size = pieces[0].shape
+    size = gram.shape[0]
     vmem = pl.BlockSpec(memory_space=pltpu.VMEM)
     return pl.pallas_call(
         factor_kernel,
-        out_shape=(
-            jax.ShapeDtypeStruct((size, size), F32),
-            pltpu.VMEM((blocks, len(pieces), line, size), F32),
-        ),
-        in_specs=[vmem if number % len(STEPS) else pl.BlockSpec(memory_space=pl.ANY) for number in range(8)]
-        + [vmem],
-        out_specs=(vmem, vmem),
-        scratch_shapes=[pltpu.SemaphoreType.DMA((8,))],
+        out_shape=pltpu.VMEM((size, size), F32),
+        in_specs=[vmem] * (len(pieces) + 1),
+        out_specs=vmem,
         name="factor",
         compiler_params=ROOM,
-    )(*(near(piece)[0] if number % len(STEPS) else piece for number, piece in enumerate(pieces)), *near(gram))
-
-
-def core_and_basis(every, inverse, moved, counts):
-    _, parts, line, size = every.shape
+    )(*near(*pieces, gram))
+
+
+def core_and_basis(pieces, inverse, moved, counts):
+    blocks, line, size = pieces[0].shape
+    parts = len(pieces)
     vmem = pl.BlockSpec(memory_space=pltpu.VMEM)
     return pl.pallas_call(
         core_kernel,
@@ -254,11 +249,15 @@
             jax.ShapeDtypeStruct((parts * line, size), F32),
             jax.ShapeDtypeStruct((128, size), BF16),
         ),
-        in_specs=[vmem, vmem, vmem, pl.BlockSpec(memory_space=pltpu.SMEM)],
+        in_specs=[vmem] * (parts + 2) + [pl.BlockSpec(memory_space=pltpu.SMEM)],
         out_specs=(vmem, vmem),
+        scratch_shapes=[
+            pltpu.VMEM((blocks, parts, line, size), F32),
+            pltpu.VMEM((parts, line, size), F32),
+        ],
         name="core",
         compiler_params=ROOM,
-    )(*near(every), inverse, *near(moved), counts)
+    )(*near(*pieces, inverse, moved), counts)
 
 
 def local(tensor_slabs, slab_counts, column_scale, samples):
@@ -279,8 +278,9 @@
     live = jnp.minimum(slab_counts, slots)
     pieces = pieces + [lax.ppermute(piece, "yz", swap) for piece in pieces]
     gram = gram_part(pieces[0], pieces[len(STEPS)])
-    inverse, every = inverse_factor(pieces, gram)
-    basis, core = core_and_basis(every, inverse, moved, live)
+    rest = [piece for number, piece in enumerate(pieces) if number % len(STEPS)]
+    inverse = inverse_factor(rest, gram)
+    basis, core = core_and_basis(pieces, inverse, moved, live)
     core = jnp.moveaxis(core.reshape(slots, -1, sketch), 2, 0)
     return basis, core
 

time: 72.2 us -> 71.4 us (0.989)
  waiting for transfers between devices: 10.2 us -> 12.2 us
  Pallas kernels: 17 us -> 15.3 us
  starting transfers between devices: 10.4 us -> 9.31 us
    ppermute x3, waiting for transfers between devices: 9.6 us -> 11.4 us  [local(): pieces.append(lax.ppermute(column, 'yz', turn))]
    pallas_call x1, Pallas kernels: 10.7 us -> 9.15 us  [inverse_factor(): pl.pallas_call(factor_kernel, out_shape=pltpu.VMEM((size, size), F32), in...]
    ppermute x3, starting transfers between devices: 4.32 us -> 3.1 us  [local(): pieces.append(lax.ppermute(column, 'yz', turn))]
  transfers between devices with their start and end apart: 8 -> 8, of which waited for: 4 -> 4; matrix products, arithmetic and copies ran while one was open for 0% -> 0% of each run, Pallas kernels for 16% -> 14%
where the time goes in v5:
time: 71.4 us; the launch traced here: 70 us
  blocking collectives  32.4 us (45%)
  Pallas kernels  15.3 us (21%)
  waiting for transfers between devices  12.2 us (17%)
  starting transfers between devices  9.31 us (13%)
    all_to_all x1, blocking collectives, local(): column = lax.all_to_all(part, 'gx', 0, 0, tiled=True)  22.5 us
    ppermute x3, waiting for transfers between devices, local(): pieces.append(lax.ppermute(column, 'yz', turn))  11.4 us
    all_to_all x1, blocking collectives, local(): lax.all_to_all(total.reshape(members, -1, sketch), 'yz', 0, 0, tiled=True)  9.88 us
    pallas_call x1, Pallas kernels, inverse_factor(): pl.pallas_call(factor_kernel, out_shape=pltpu.VMEM((size, size), F32), in...  9.15 us
    all_to_all x1, starting transfers between devices, local(): moved = lax.all_to_all(chunks, 'gx', 0, 0, tiled=True)  5.7 us
    ppermute x3, starting transfers between devices, local(): pieces.append(lax.ppermute(column, 'yz', turn))  3.1 us
    pallas_call x1, Pallas kernels, sketch_parts(): pl.pallas_call(sketch_kernel, out_shape=(pltpu.VMEM((rows, sketch), F32),...  2.87 us
    pallas_call x1, Pallas kernels, core_and_basis(): pl.pallas_call(core_kernel, out_shape=(jax.ShapeDtypeStruct((parts * line...  2.74 us
  transfers between devices with their start and end apart: 8, of which 4 were waited for; matrix products, arithmetic and copies ran while one was open for 0% of the time, Pallas kernels for 14%

profile of v5, /device:TPU:2, one launch (start us, length us, event | category | flops | bytes accessed | tf_op | source)
XLA Modules:
  0.0 70.0 jit_solution(9728261363714706731)
XLA Ops:
  0.6 2.9 %sketch.1 = (f32[64,256]{1,0:T(8,128)S(1)}, bf16[32,64,128]{2,1,0:T(8,128)(2,1)}) custom-call(bf16[64,4,1024]{2,1,0:T(4,128)(2,1)} %tensor_ref.1, s32[8]{0:T(128)} %counts_ref.1, f32[16,1024]{1,0:T(8,128)} %scale_ref.1, s32[16,256]{1,0:T(8,128)} %samples_ref.1), custom_call_target="tpu_custom_call" | custom-call | tf_op jit(solution)/shard_map/sketch/pallas_call | solution.py:76
  3.5 9.9 %all_to_all.15 = f32[8,8,256]{2,1,0:T(8,128)S(1)} all-to-all(f32[8,8,256]{2,1,0:T(8,128)S(1)} %bitcast.4), channel_id=1, replica_groups=mesh['gx'=32,'yz'=8] {'yz'}, dimensions={0} | all-to-all | bytes 131072 | tf_op jit(solution)/shard_map/all_to_all | solution.py:270
  13.4 22.5 %all_to_all.16.refs_0_ = f32[32,8,256]{2,1,0:T(8,128)S(1)} all-to-all(f32[32,8,256]{2,1,0:T(8,128)S(1)} %broadcast_in_dim.3), channel_id=1, replica_groups=mesh['gx'=32,'yz'=8] {'gx'}, dimensions={0} | all-to-all | bytes 524288 | tf_op jit(solution)/shard_map/all_to_all | solution.py:272
  35.9 0.0 copy-start
  35.9 5.7 %all-to-all-start.2 = ((bf16[32,64,128]{2,1,0:T(8,128)(2,1)}), bf16[32,64,128]{2,1,0:T(8,128)(2,1)S(1)}, u32[]{:S(2)}, u32[]{:S(2)}) async-start(bf16[32,64,128]{2,1,0:T(8,128)(2,1)} %get-tuple-element.7), calls=%async_computation.2 | async-start | bytes 1048576 | tf_op jit(solution)/shard_map/all_to_all | solution.py:277
  41.7 1.2 %collective-permute-start.2 = (f32[32,8,256]{2,1,0:T(8,128)S(1)}, f32[32,8,256]{2,1,0:T(8,128)S(1)}, u32[]{:S(2)}, u32[]{:S(2)}) collective-permute-start(f32[32,8,256]{2,1,0:T(8,128)S(1)} %all_to_all.16.refs_0_), channel_id=1, source_target_pairs={{0,6},{1,7},{2,0},{3,1},{4,2},{5,3},{6,4},{7,5},{8,14},{9,15},{10,... | collective-permute-start | bytes 786440 | tf_op jit(solution)/shard_map/ppermute | solution.py:276
  42.9 0.9 %collective-permute-start.1 = (f32[32,8,256]{2,1,0:T(8,128)S(1)}, f32[32,8,256]{2,1,0:T(8,128)S(1)}, u32[]{:S(2)}, u32[]{:S(2)}) collective-permute-start(f32[32,8,256]{2,1,0:T(8,128)S(1)} %all_to_all.16.refs_0_), channel_id=1, source_target_pairs={{0,2},{1,3},{2,4},{3,5},{4,6},{5,7},{6,0},{7,1},{8,10},{9,11},{10,... | collective-permute-start | bytes 786440 | tf_op jit(solution)/shard_map/ppermute | solution.py:276
  43.8 1.0 %collective-permute-start = (f32[32,8,256]{2,1,0:T(8,128)S(1)}, f32[32,8,256]{2,1,0:T(8,128)S(1)}, u32[]{:S(2)}, u32[]{:S(2)}) collective-permute-start(f32[32,8,256]{2,1,0:T(8,128)S(1)} %all_to_all.16.refs_0_), channel_id=1, source_target_pairs={{0,4},{1,5},{2,6},{3,7},{4,0},{5,1},{6,2},{7,3},{8,12},{9,13},{10,... | collective-permute-start | bytes 786440 | tf_op jit(solution)/shard_map/ppermute | solution.py:276
  44.8 0.0 collective-permute-start.3
  44.8 6.2 %collective-permute-done.2.refs_2_.refs_3_ = f32[32,8,256]{2,1,0:T(8,128)S(1)} collective-permute-done((f32[32,8,256]{2,1,0:T(8,128)S(1)}, f32[32,8,256]{2,1,0:T(8,128)S(1)}, u32[]{:S(2)}, u32[]{:S(2)}) %collective-permute-start.2) | collective-permute-done | bytes 262176 | tf_op jit(solution)/shard_map/ppermute | solution.py:276
  50.9 0.0 collective-permute-start.6
  50.9 5.2 %collective-permute-done.1.refs_1_.refs_2_ = f32[32,8,256]{2,1,0:T(8,128)S(1)} collective-permute-done((f32[32,8,256]{2,1,0:T(8,128)S(1)}, f32[32,8,256]{2,1,0:T(8,128)S(1)}, u32[]{:S(2)}, u32[]{:S(2)}) %collective-permute-start.1) | collective-permute-done | bytes 262176 | tf_op jit(solution)/shard_map/ppermute | solution.py:276
  56.2 0.0 collective-permute-start.5
  56.2 0.0 collective-permute-done.refs_0_.refs_1_
  56.2 0.5 collective-permute-start.4
  56.7 0.0 copy-done
  56.7 0.0 collective-permute-done.3.refs_1_.refs_4_
  56.7 0.5 gram.1.refs_6_
  57.2 0.0 collective-permute-done.6.refs_5_.refs_7_
  57.2 0.5 collective-permute-done.5.refs_4_.refs_6_
  57.7 0.4 collective-permute-done.4.refs_3_.refs_5_
  58.1 9.1 %factor.1.refs_8_ = f32[256,256]{1,0:T(8,128)S(1)} custom-call(f32[32,8,256]{2,1,0:T(8,128)S(1)} %collective-permute-done.refs_0_.refs_1_, f32[32,8,256]{2,1,0:T(8,128)S(1)} %collective-permute-done.1.refs_1_.refs_2_, f32[32,8,256]{2,1,0:T(8,128)S(1)} %collective-permute-done.2.refs_2_.refs_3_, f32[32,8,256]{2,1,0:T(8,128)S(1)} %collective-permute-done.4.refs_3_.refs_5_, ...), custom_call_target="tpu_custom_call" | custom-call | tf_op jit(solution)/shard_map/factor/pallas_call | solution.py:232
  67.2 0.0 all-to-all-done.2.refs_9_
  67.2 2.7 %core.1 = (f32[64,256]{1,0:T(8,128)}, bf16[128,256]{1,0:T(8,128)(2,1)}) custom-call(f32[32,8,256]{2,1,0:T(8,128)S(1)} %all_to_all.16.refs_0_, f32[32,8,256]{2,1,0:T(8,128)S(1)} %collective-permute-done.refs_0_.refs_1_, f32[32,8,256]{2,1,0:T(8,128)S(1)} %collective-permute-done.1.refs_1_.refs_2_, f32[32,8,256]{2,1,0:T(8,128)S(1)} %collective-permute-done.2.refs_2_.refs_3_, ...), custom_call_target="tpu_custom_call" | custom-call | tf_op jit(solution)/shard_map/core/pallas_call | solution.py:246
  (3 shorter events, 0.0 us)
Async XLA Ops:
  35.9 20.7 %copy-start = (s32[8]{0:T(128)S(1)}, s32[8]{0:T(128)}, u32[]{:S(2)}) copy-start(s32[8]{0:T(128)} %counts_ref.1) | copy-start | bytes 100
  35.9 31.3 %all-to-all-start.2 = ((bf16[32,64,128]{2,1,0:T(8,128)(2,1)}), bf16[32,64,128]{2,1,0:T(8,128)(2,1)S(1)}, u32[]{:S(2)}, u32[]{:S(2)}) async-start(bf16[32,64,128]{2,1,0:T(8,128)(2,1)} %get-tuple-element.7), calls=%async_computation.2 | async-start | bytes 1048576 | tf_op jit(solution)/shard_map/all_to_all | solution.py:277
  41.7 9.3 %collective-permute-start.2 = (f32[32,8,256]{2,1,0:T(8,128)S(1)}, f32[32,8,256]{2,1,0:T(8,128)S(1)}, u32[]{:S(2)}, u32[]{:S(2)}) collective-permute-start(f32[32,8,256]{2,1,0:T(8,128)S(1)} %all_to_all.16.refs_0_), channel_id=1, source_target_pairs={{0,6},{1,7},{2,0},{3,1},{4,2},{5,3},{6,4},{7,5},{8,14},{9,15},{10,... | collective-permute-start | bytes 786440 | tf_op jit(solution)/shard_map/ppermute | solution.py:276
  42.9 13.3 %collective-permute-start.1 = (f32[32,8,256]{2,1,0:T(8,128)S(1)}, f32[32,8,256]{2,1,0:T(8,128)S(1)}, u32[]{:S(2)}, u32[]{:S(2)}) collective-permute-start(f32[32,8,256]{2,1,0:T(8,128)S(1)} %all_to_all.16.refs_0_), channel_id=1, source_target_pairs={{0,2},{1,3},{2,4},{3,5},{4,6},{5,7},{6,0},{7,1},{8,10},{9,11},{10,... | collective-permute-start | bytes 786440 | tf_op jit(solution)/shard_map/ppermute | solution.py:276
  43.8 12.4 %collective-permute-start = (f32[32,8,256]{2,1,0:T(8,128)S(1)}, f32[32,8,256]{2,1,0:T(8,128)S(1)}, u32[]{:S(2)}, u32[]{:S(2)}) collective-permute-start(f32[32,8,256]{2,1,0:T(8,128)S(1)} %all_to_all.16.refs_0_), channel_id=1, source_target_pairs={{0,4},{1,5},{2,6},{3,7},{4,0},{5,1},{6,2},{7,3},{8,12},{9,13},{10,... | collective-permute-start | bytes 786440 | tf_op jit(solution)/shard_map/ppermute | solution.py:276
  44.8 11.9 %collective-permute-start.3 = (f32[32,8,256]{2,1,0:T(8,128)S(1)}, f32[32,8,256]{2,1,0:T(8,128)S(1)}, u32[]{:S(2)}, u32[]{:S(2)}) collective-permute-start(f32[32,8,256]{2,1,0:T(8,128)S(1)} %all_to_all.16.refs_0_), channel_id=1, source_target_pairs={{0,1},{1,0},{2,3},{3,2},{4,5},{5,4},{6,7},{7,6},{8,9},{9,8},{10,11... | collective-permute-start | bytes 786440 | tf_op jit(solution)/shard_map/ppermute | solution.py:279
  50.9 6.3 %collective-permute-start.6 = (f32[32,8,256]{2,1,0:T(8,128)S(1)}, f32[32,8,256]{2,1,0:T(8,128)S(1)}, u32[]{:S(2)}, u32[]{:S(2)}) collective-permute-start(f32[32,8,256]{2,1,0:T(8,128)S(1)} %collective-permute-done.2.refs_2_.refs_3_), channel_id=1, source_target_pairs={{0,1},{1,0},{2,3},{3,2},{4,5},{5,4},{6,7},{7,6},{8,9},{9,8},{10,11... | collective-permute-start | bytes 786440 | tf_op jit(solution)/shard_map/ppermute | solution.py:279
  56.2 1.5 %collective-permute-start.5 = (f32[32,8,256]{2,1,0:T(8,128)S(1)}, f32[32,8,256]{2,1,0:T(8,128)S(1)}, u32[]{:S(2)}, u32[]{:S(2)}) collective-permute-start(f32[32,8,256]{2,1,0:T(8,128)S(1)} %collective-permute-done.1.refs_1_.refs_2_), channel_id=1, source_target_pairs={{0,1},{1,0},{2,3},{3,2},{4,5},{5,4},{6,7},{7,6},{8,9},{9,8},{10,11... | collective-permute-start | bytes 786440 | tf_op jit(solution)/shard_map/ppermute | solution.py:279
  56.2 1.9 %collective-permute-start.4 = (f32[32,8,256]{2,1,0:T(8,128)S(1)}, f32[32,8,256]{2,1,0:T(8,128)S(1)}, u32[]{:S(2)}, u32[]{:S(2)}) collective-permute-start(f32[32,8,256]{2,1,0:T(8,128)S(1)} %collective-permute-done.refs_0_.refs_1_), channel_id=1, source_target_pairs={{0,1},{1,0},{2,3},{3,2},{4,5},{5,4},{6,7},{7,6},{8,9},{9,8},{10,11... | collective-permute-start | bytes 786440 | tf_op jit(solution)/shard_map/ppermute | solution.py:279

commit v6 on v5

--- a/solution.py
+++ b/solution.py
@@ -9,7 +9,7 @@
 F32, BF16, I32 = jnp.float32, jnp.bfloat16, jnp.int32
 NN, NT, TN = ((1,), (0,)), ((1,), (1,)), ((0,), (0,))
 HIGHEST = lax.Precision.HIGHEST
-AHEAD = 10
+AHEAD = 9
 BLOCK = 64
 STEPS = (0, 2, 1, 3)
 SLOTS = 4
@@ -37,24 +37,37 @@
     return offset, counts_ref[index]
 
 
-def sketch_kernel(tensor_ref, counts_ref, scale_ref, samples_ref, total_ref, moved_ref, hadamard_ref):
+def sketch_kernel(tensor_any, counts_ref, scale_any, samples_any, total_ref, moved_ref,
+                  tensor_ref, scale_ref, samples_ref, hadamard_ref, sems):
+    copies = [
+        pltpu.make_async_copy(source, target, sems.at[number])
+        for number, (source, target) in enumerate(
+            ((samples_any, samples_ref), (tensor_any, tensor_ref), (scale_any, scale_ref))
+        )
+    ]
+    for copy in copies:
+        copy.start()
     rows, slots, width = tensor_ref.shape
     total_slabs, sketch = samples_ref.shape
     index = lax.axis_index("yz")
     offset, count = own_slabs(counts_ref, index, counts_ref.shape[0])
+    slabs = [jnp.minimum(offset + slot, total_slabs - 1) for slot in range(slots)]
+    copies[0].wait()
+    for slot, slab in enumerate(slabs):
+        picked = samples_ref[pl.ds(slab, 1), :]
+        low = signs(32, picked & 31)
+        high = signs(width // 32, picked >> 5)
+        for part in range(width // 32):
+            hadamard_ref[slot, pl.ds(part * 32, 32), :] = (low * high[part : part + 1, :]).astype(BF16)
+    copies[1].wait()
     lines = tensor_ref[...].astype(F32).reshape(rows * slots, width).astype(BF16)
     at = lax.broadcasted_iota(I32, (rows * slots, rows * slots), 0)
     of = lax.broadcasted_iota(I32, (rows * slots, rows * slots), 1)
     pick = ((at % rows) * slots + at // rows == of).astype(F32).astype(BF16)
     by_slot = dot(pick, lines, NN)
+    copies[2].wait()
     total = jnp.zeros((rows, sketch), F32)
-    for slot in range(slots):
-        slab = jnp.minimum(offset + slot, total_slabs - 1)
-        picked = samples_ref[pl.ds(slab, 1), :]
-        low = signs(32, picked & 31)
-        high = signs(width // 32, picked >> 5)
-        for part in range(width // 32):
-            hadamard_ref[slot, pl.ds(part * 32, 32), :] = (low * high[part : part + 1, :]).astype(BF16)
+    for slot, slab in enumerate(slabs):
         piece = by_slot[slot * rows : (slot + 1) * rows]
         scaled = (piece * scale_ref[pl.ds(slab, 1), :]).astype(BF16)
         term = dot(scaled, hadamard_ref[slot], NN)
@@ -73,28 +86,35 @@
     sketch = samples.shape[1]
     chunks = width * slots // 128
     vmem = pl.BlockSpec(memory_space=pltpu.VMEM)
+    free = pl.BlockSpec(memory_space=pl.ANY)
     return pl.pallas_call(
         sketch_kernel,
         out_shape=(pltpu.VMEM((rows, sketch), F32), jax.ShapeDtypeStruct((chunks, rows, 128), BF16)),
-        in_specs=[vmem, pl.BlockSpec(memory_space=pltpu.SMEM), vmem, vmem],
+        in_specs=[free, pl.BlockSpec(memory_space=pltpu.SMEM), free, free],
         out_specs=(vmem, vmem),
-        scratch_shapes=[pltpu.VMEM((slots, width, sketch), BF16)],
+        scratch_shapes=[
+            pltpu.VMEM(tensor.shape, tensor.dtype),
+            pltpu.VMEM(scale.shape, scale.dtype),
+            pltpu.VMEM(samples.shape, samples.dtype),
+            pltpu.VMEM((slots, width, sketch), BF16),
+            pltpu.SemaphoreType.DMA((3,)),
+        ],
         name="sketch",
     )(tensor, counts, scale, samples)
 
 
-def block_inverse(tiles):
+def block_inverse(tiles, first):
     count = len(tiles)
     size = 8 * count
     lines = list(tiles)
     sub = lax.broadcasted_iota(I32, (8, 128), 0)
-    lane = lax.broadcasted_iota(I32, (8, 128), 1)
+    lane = lax.broadcasted_iota(I32, (8, 128), 1) - first
 
     def row_of(tile, at):
         return jnp.broadcast_to(tile[at : at + 1, :], (8, 128))
 
     def column_of(tile, at):
-        return jnp.broadcast_to(tile[:, at : at + 1], (8, 128))
+        return jnp.broadcast_to(tile[:, first + at : first + at + 1], (8, 128))
 
     columns = {j: [column_of(tile, j) for tile in lines] for j in range(min(AHEAD, size))}
     pivots = [jnp.ones((8, 128), F32)] * count
@@ -120,39 +140,39 @@
             lines[t] = jnp.where(cleared, 0.0, lines[t]) - factor * line
         new = step + AHEAD
         if new < size:
-            columns[new] = [
-                column_of(lines[t], new) if t >= (step + 1) // 8 else None for t in range(count)
-            ]
+            columns[new] = [column_of(lines[t], new) if t >= (step + 1) // 8 else None for t in range(count)]
     result = []
     for t in range(count):
         inside = jnp.where(lane == sub + 8 * t, 1.0, 0.0)
-        result.append(lax.rsqrt(pivots[t]) * jnp.where(lane < sub + 8 * t, lines[t], inside))
+        inside = jnp.where((lane >= 0) & (lane < sub + 8 * t), lines[t], inside)
+        result.append(lax.rsqrt(pivots[t]) * inside)
     return jnp.concatenate(result, 0)
 
 
 def invert_factor(work_ref):
     size = work_ref.shape[0]
     lanes = lax.broadcasted_iota(I32, (1, size), 1)
-
-    def spread(block):
-        return jnp.concatenate([block, jnp.zeros((BLOCK, 128 - BLOCK), F32)], 1)
-
-    diagonal = spread(work_ref[0:BLOCK, 0:BLOCK])
+    block = work_ref[0:BLOCK, 0:128]
     for start in range(0, size, BLOCK):
         end = start + BLOCK
         after = end + BLOCK
-        inverse = block_inverse([diagonal[8 * t : 8 * t + 8] for t in range(BLOCK // 8)])[:, :BLOCK]
+        group = start // 128 * 128
+        first = start - group
+        inverse = block_inverse([block[8 * t : 8 * t + 8] for t in range(BLOCK // 8)], first)
+        here = (lanes >= start) & (lanes < end)
+        placed = [jnp.zeros((BLOCK, 128), F32)] * (size // 128)
+        placed[group // 128] = inverse
+        line = jnp.where(here, jnp.concatenate(placed, 1), dot(inverse, work_ref[group : group + 128, :], NN, HIGHEST))
         if end < size:
-            below = dot(work_ref[end:after, start:end], inverse, NT, HIGHEST)
-            diagonal = spread(work_ref[end:after, end:after] - dot(below, below, NT, HIGHEST))
-            rest = dot(work_ref[end:, start:end], inverse, NT, HIGHEST)
-        work_ref[start:end, :] = dot(inverse, work_ref[start:end, :], NN, HIGHEST)
-        work_ref[start:end, start:end] = inverse
+            below = dot(work_ref[end:after, group : group + 128], inverse, NT, HIGHEST)
+            new = jnp.where(here, 0.0, work_ref[end:after, :]) - dot(below, line, NN, HIGHEST)
+            block = new[:, end // 128 * 128 : end // 128 * 128 + 128]
+        if after < size:
+            rest = dot(work_ref[after:, group : group + 128], inverse, NT, HIGHEST)
+            work_ref[after:, :] = jnp.where(here, 0.0, work_ref[after:, :]) - dot(rest, line, NN, HIGHEST)
+        work_ref[start:end, :] = line
         if end < size:
-            here = (lanes >= start) & (lanes < end)
-            work_ref[end:, :] = jnp.where(here, 0.0, work_ref[end:, :]) - dot(
-                rest, work_ref[start:end, :], NN, HIGHEST
-            )
+            work_ref[end:after, :] = new
     row = lax.broadcasted_iota(I32, (size, size), 0)
     column = lax.broadcasted_iota(I32, (size, size), 1)
     work_ref[...] = jnp.where(row >= column, work_ref[...], 0.0)

time: 71.4 us -> 71.8 us (level)
  the two profiles are of different devices: /device:TPU:2 before, /device:TPU:1 now
where the time goes in v6:
time: 71.8 us; the launch traced here: 71.4 us
  blocking collectives  32.7 us (46%)
  starting transfers between devices  20 us (28%)
  Pallas kernels  15.6 us (22%)
  waiting for transfers between devices  2.35 us (3%)
    all_to_all x1, blocking collectives, local(): column = lax.all_to_all(part, 'gx', 0, 0, tiled=True)  22.1 us
    ppermute x4, starting transfers between devices, local(): pieces = pieces + [lax.ppermute(piece, 'yz', swap) for piece in pieces]  12.9 us
    all_to_all x1, blocking collectives, local(): lax.all_to_all(total.reshape(members, -1, sketch), 'yz', 0, 0, tiled=True)  10.6 us
    pallas_call x1, Pallas kernels, inverse_factor(): pl.pallas_call(factor_kernel, out_shape=pltpu.VMEM((size, size), F32), in...  8.85 us
    all_to_all x1, starting transfers between devices, local(): moved = lax.all_to_all(chunks, 'gx', 0, 0, tiled=True)  4.87 us
    pallas_call x1, Pallas kernels, sketch_parts(): pl.pallas_call(sketch_kernel, out_shape=(pltpu.VMEM((rows, sketch), F32),...  3.51 us
    pallas_call x1, Pallas kernels, core_and_basis(): pl.pallas_call(core_kernel, out_shape=(jax.ShapeDtypeStruct((parts * line...  2.73 us
    ppermute x3, starting transfers between devices, local(): pieces.append(lax.ppermute(column, 'yz', turn))  2.26 us
  transfers between devices with their start and end apart: 8, of which 3 were waited for; matrix products, arithmetic and copies ran while one was open for 0% of the time, Pallas kernels for 13%

profile of v6, /device:TPU:1, one launch (start us, length us, event | category | flops | bytes accessed | tf_op | source)
XLA Modules:
  0.0 71.4 jit_solution(4177264942676560599)
XLA Ops:
  0.6 3.5 %sketch.1 = (f32[64,256]{1,0:T(8,128)S(1)}, bf16[32,64,128]{2,1,0:T(8,128)(2,1)}) custom-call(bf16[64,4,1024]{2,1,0:T(4,128)(2,1)} %tensor_any.1, s32[8]{0:T(128)} %counts_ref.1, f32[16,1024]{1,0:T(8,128)} %scale_any.1, s32[16,256]{1,0:T(8,128)} %samples_any.1), custom_call_target="tpu_custom_call" | custom-call | tf_op jit(solution)/shard_map/sketch/pallas_call | solution.py:90
  4.2 10.6 %all_to_all.15 = f32[8,8,256]{2,1,0:T(8,128)S(1)} all-to-all(f32[8,8,256]{2,1,0:T(8,128)S(1)} %bitcast.4), channel_id=1, replica_groups=mesh['gx'=32,'yz'=8] {'yz'}, dimensions={0} | all-to-all | bytes 131072 | tf_op jit(solution)/shard_map/all_to_all | solution.py:290
  14.8 22.1 %all_to_all.16.refs_0_ = f32[32,8,256]{2,1,0:T(8,128)S(1)} all-to-all(f32[32,8,256]{2,1,0:T(8,128)S(1)} %broadcast_in_dim.3), channel_id=1, replica_groups=mesh['gx'=32,'yz'=8] {'gx'}, dimensions={0} | all-to-all | bytes 524288 | tf_op jit(solution)/shard_map/all_to_all | solution.py:292
  36.9 0.0 copy-start
  36.9 4.9 %all-to-all-start.2 = ((bf16[32,64,128]{2,1,0:T(8,128)(2,1)}), bf16[32,64,128]{2,1,0:T(8,128)(2,1)S(1)}, u32[]{:S(2)}, u32[]{:S(2)}) async-start(bf16[32,64,128]{2,1,0:T(8,128)(2,1)} %get-tuple-element.7), calls=%async_computation.2 | async-start | bytes 1048576 | tf_op jit(solution)/shard_map/all_to_all | solution.py:297
  41.8 1.0 %collective-permute-start.2 = (f32[32,8,256]{2,1,0:T(8,128)S(1)}, f32[32,8,256]{2,1,0:T(8,128)S(1)}, u32[]{:S(2)}, u32[]{:S(2)}) collective-permute-start(f32[32,8,256]{2,1,0:T(8,128)S(1)} %all_to_all.16.refs_0_), channel_id=1, source_target_pairs={{0,6},{1,7},{2,0},{3,1},{4,2},{5,3},{6,4},{7,5},{8,14},{9,15},{10,... | collective-permute-start | bytes 786440 | tf_op jit(solution)/shard_map/ppermute | solution.py:296
  42.7 0.6 collective-permute-start.1
  43.3 0.7 collective-permute-start
  44.0 2.6 %collective-permute-start.3 = (f32[32,8,256]{2,1,0:T(8,128)S(1)}, f32[32,8,256]{2,1,0:T(8,128)S(1)}, u32[]{:S(2)}, u32[]{:S(2)}) collective-permute-start(f32[32,8,256]{2,1,0:T(8,128)S(1)} %all_to_all.16.refs_0_), channel_id=1, source_target_pairs={{0,1},{1,0},{2,3},{3,2},{4,5},{5,4},{6,7},{7,6},{8,9},{9,8},{10,11... | collective-permute-start | bytes 786440 | tf_op jit(solution)/shard_map/ppermute | solution.py:299
  46.6 1.4 %collective-permute-done.2.refs_2_.refs_3_ = f32[32,8,256]{2,1,0:T(8,128)S(1)} collective-permute-done((f32[32,8,256]{2,1,0:T(8,128)S(1)}, f32[32,8,256]{2,1,0:T(8,128)S(1)}, u32[]{:S(2)}, u32[]{:S(2)}) %collective-permute-start.2) | collective-permute-done | bytes 262176 | tf_op jit(solution)/shard_map/ppermute | solution.py:296
  48.0 4.8 %collective-permute-start.6 = (f32[32,8,256]{2,1,0:T(8,128)S(1)}, f32[32,8,256]{2,1,0:T(8,128)S(1)}, u32[]{:S(2)}, u32[]{:S(2)}) collective-permute-start(f32[32,8,256]{2,1,0:T(8,128)S(1)} %collective-permute-done.2.refs_2_.refs_3_), channel_id=1, source_target_pairs={{0,1},{1,0},{2,3},{3,2},{4,5},{5,4},{6,7},{7,6},{8,9},{9,8},{10,11... | collective-permute-start | bytes 786440 | tf_op jit(solution)/shard_map/ppermute | solution.py:299
  52.8 0.0 collective-permute-done.1.refs_1_.refs_2_
  52.8 5.5 %collective-permute-start.5 = (f32[32,8,256]{2,1,0:T(8,128)S(1)}, f32[32,8,256]{2,1,0:T(8,128)S(1)}, u32[]{:S(2)}, u32[]{:S(2)}) collective-permute-start(f32[32,8,256]{2,1,0:T(8,128)S(1)} %collective-permute-done.1.refs_1_.refs_2_), channel_id=1, source_target_pairs={{0,1},{1,0},{2,3},{3,2},{4,5},{5,4},{6,7},{7,6},{8,9},{9,8},{10,11... | collective-permute-start | bytes 786440 | tf_op jit(solution)/shard_map/ppermute | solution.py:299
  58.3 0.0 collective-permute-done.refs_0_.refs_1_
  58.3 0.0 collective-permute-start.4
  58.3 0.0 copy-done
  58.3 0.0 collective-permute-done.3.refs_1_.refs_4_
  58.3 0.5 gram.1.refs_6_
  58.9 0.0 collective-permute-done.6.refs_5_.refs_7_
  58.9 0.6 collective-permute-done.5.refs_4_.refs_6_
  59.5 0.4 collective-permute-done.4.refs_3_.refs_5_
  59.8 8.8 %factor.1.refs_8_ = f32[256,256]{1,0:T(8,128)S(1)} custom-call(f32[32,8,256]{2,1,0:T(8,128)S(1)} %collective-permute-done.refs_0_.refs_1_, f32[32,8,256]{2,1,0:T(8,128)S(1)} %collective-permute-done.1.refs_1_.refs_2_, f32[32,8,256]{2,1,0:T(8,128)S(1)} %collective-permute-done.2.refs_2_.refs_3_, f32[32,8,256]{2,1,0:T(8,128)S(1)} %collective-permute-done.4.refs_3_.refs_5_, ...), custom_call_target="tpu_custom_call" | custom-call | tf_op jit(solution)/shard_map/factor/pallas_call | solution.py:252
  68.7 0.0 all-to-all-done.2.refs_9_
  68.7 2.7 %core.1 = (f32[64,256]{1,0:T(8,128)}, bf16[128,256]{1,0:T(8,128)(2,1)}) custom-call(f32[32,8,256]{2,1,0:T(8,128)S(1)} %all_to_all.16.refs_0_, f32[32,8,256]{2,1,0:T(8,128)S(1)} %collective-permute-done.refs_0_.refs_1_, f32[32,8,256]{2,1,0:T(8,128)S(1)} %collective-permute-done.1.refs_1_.refs_2_, f32[32,8,256]{2,1,0:T(8,128)S(1)} %collective-permute-done.2.refs_2_.refs_3_, ...), custom_call_target="tpu_custom_call" | custom-call | tf_op jit(solution)/shard_map/core/pallas_call | solution.py:266
  (3 shorter events, 0.0 us)
Async XLA Ops:
  36.9 21.4 %copy-start = (s32[8]{0:T(128)S(1)}, s32[8]{0:T(128)}, u32[]{:S(2)}) copy-start(s32[8]{0:T(128)} %counts_ref.1) | copy-start | bytes 100
  36.9 31.8 %all-to-all-start.2 = ((bf16[32,64,128]{2,1,0:T(8,128)(2,1)}), bf16[32,64,128]{2,1,0:T(8,128)(2,1)S(1)}, u32[]{:S(2)}, u32[]{:S(2)}) async-start(bf16[32,64,128]{2,1,0:T(8,128)(2,1)} %get-tuple-element.7), calls=%async_computation.2 | async-start | bytes 1048576 | tf_op jit(solution)/shard_map/all_to_all | solution.py:297
  41.8 6.2 %collective-permute-start.2 = (f32[32,8,256]{2,1,0:T(8,128)S(1)}, f32[32,8,256]{2,1,0:T(8,128)S(1)}, u32[]{:S(2)}, u32[]{:S(2)}) collective-permute-start(f32[32,8,256]{2,1,0:T(8,128)S(1)} %all_to_all.16.refs_0_), channel_id=1, source_target_pairs={{0,6},{1,7},{2,0},{3,1},{4,2},{5,3},{6,4},{7,5},{8,14},{9,15},{10,... | collective-permute-start | bytes 786440 | tf_op jit(solution)/shard_map/ppermute | solution.py:296
  42.7 10.0 %collective-permute-start.1 = (f32[32,8,256]{2,1,0:T(8,128)S(1)}, f32[32,8,256]{2,1,0:T(8,128)S(1)}, u32[]{:S(2)}, u32[]{:S(2)}) collective-permute-start(f32[32,8,256]{2,1,0:T(8,128)S(1)} %all_to_all.16.refs_0_), channel_id=1, source_target_pairs={{0,2},{1,3},{2,4},{3,5},{4,6},{5,7},{6,0},{7,1},{8,10},{9,11},{10,... | collective-permute-start | bytes 786440 | tf_op jit(solution)/shard_map/ppermute | solution.py:296
  43.3 15.0 %collective-permute-start = (f32[32,8,256]{2,1,0:T(8,128)S(1)}, f32[32,8,256]{2,1,0:T(8,128)S(1)}, u32[]{:S(2)}, u32[]{:S(2)}) collective-permute-start(f32[32,8,256]{2,1,0:T(8,128)S(1)} %all_to_all.16.refs_0_), channel_id=1, source_target_pairs={{0,4},{1,5},{2,6},{3,7},{4,0},{5,1},{6,2},{7,3},{8,12},{9,13},{10,... | collective-permute-start | bytes 786440 | tf_op jit(solution)/shard_map/ppermute | solution.py:296
  44.0 14.3 %collective-permute-start.3 = (f32[32,8,256]{2,1,0:T(8,128)S(1)}, f32[32,8,256]{2,1,0:T(8,128)S(1)}, u32[]{:S(2)}, u32[]{:S(2)}) collective-permute-start(f32[32,8,256]{2,1,0:T(8,128)S(1)} %all_to_all.16.refs_0_), channel_id=1, source_target_pairs={{0,1},{1,0},{2,3},{3,2},{4,5},{5,4},{6,7},{7,6},{8,9},{9,8},{10,11... | collective-permute-start | bytes 786440 | tf_op jit(solution)/shard_map/ppermute | solution.py:299
  48.0 10.9 %collective-permute-start.6 = (f32[32,8,256]{2,1,0:T(8,128)S(1)}, f32[32,8,256]{2,1,0:T(8,128)S(1)}, u32[]{:S(2)}, u32[]{:S(2)}) collective-permute-start(f32[32,8,256]{2,1,0:T(8,128)S(1)} %collective-permute-done.2.refs_2_.refs_3_), channel_id=1, source_target_pairs={{0,1},{1,0},{2,3},{3,2},{4,5},{5,4},{6,7},{7,6},{8,9},{9,8},{10,11... | collective-permute-start | bytes 786440 | tf_op jit(solution)/shard_map/ppermute | solution.py:299
  52.8 6.7 %collective-permute-start.5 = (f32[32,8,256]{2,1,0:T(8,128)S(1)}, f32[32,8,256]{2,1,0:T(8,128)S(1)}, u32[]{:S(2)}, u32[]{:S(2)}) collective-permute-start(f32[32,8,256]{2,1,0:T(8,128)S(1)} %collective-permute-done.1.refs_1_.refs_2_), channel_id=1, source_target_pairs={{0,1},{1,0},{2,3},{3,2},{4,5},{5,4},{6,7},{7,6},{8,9},{9,8},{10,11... | collective-permute-start | bytes 786440 | tf_op jit(solution)/shard_map/ppermute | solution.py:299
  58.3 1.5 %collective-permute-start.4 = (f32[32,8,256]{2,1,0:T(8,128)S(1)}, f32[32,8,256]{2,1,0:T(8,128)S(1)}, u32[]{:S(2)}, u32[]{:S(2)}) collective-permute-start(f32[32,8,256]{2,1,0:T(8,128)S(1)} %collective-permute-done.refs_0_.refs_1_), channel_id=1, source_target_pairs={{0,1},{1,0},{2,3},{3,2},{4,5},{5,4},{6,7},{7,6},{8,9},{9,8},{10,11... | collective-permute-start | bytes 786440 | tf_op jit(solution)/shard_map/ppermute | solution.py:299
